TPU v7x, 32 devices: a whole 2x2x4 slice. The times are simulated.
32 devices in a mesh: tm: 4 (over z), query: 2 (over y), rec: 4 (over x, core).
Axes of the slice: x: 2, y: 2, z: 4, core: 2. Of those that a mesh axis runs over, the one named last changes fastest.
Arguments:
- frames: bfloat16 [4, 2048, 1024], P('rec', 'tm'), may hold values from -100 to 100
- queries: bfloat16 [4096, 1024], P('query'), may hold values from -10 to 10
- kernel: float32 [33, 4096], P(None, 'query'), may hold values from 0.01 to 0.12
- labels: int32 [4, 2048], P('rec', 'tm'), may hold values from 0 to 4095
- lengths: int32 [4], P('rec'), may hold values from 512 to 2048, as said below
Outputs:
- grad_frames: bfloat16 [4, 2048, 1024], P('rec', 'tm', 'query')
- grad_queries: bfloat16 [4096, 1024], P('query', 'rec')
- grad_kernel: float32 [33, 4096], P(None, 'query')
Inputs may be any that keep to these rules, and one draw needn't show every extreme that they name: `lengths`: each entry counts the valid frames at the start of its recording; at least one recording has all 2048 frames valid.
All inputs are finite; a program needn't handle non-finite values.
Results may differ from a plain program's by a relative error of at most 0.0049.
Values sent between devices are 32-bit elements; how exact they have to be, the bound alone decides.
A program may use at most 64 MiB of HBM per device.

v0:
```python
import math

import jax
import jax.numpy as jnp
from jax import lax
from jax.sharding import PartitionSpec as P


def merged(x, axis, combine):
    everything = jax.tree.map(lambda part: lax.all_gather(part, axis), x)
    first = jax.tree.map(lambda part: part[0], everything)

    def step(k, so_far):
        return combine(so_far, jax.tree.map(lambda part: part[k], everything))

    return lax.fori_loop(1, lax.axis_size(axis), step, first)


def with_halo(x, sides, width):
    for axis, dim in sides:
        peers, length = (lax.axis_size(axis), x.shape[dim])
        up = [(i, (i + 1) % peers) for i in range(peers - 1)]
        down = [(j, i) for i, j in up]
        last = lax.slice_in_dim(x, length - width, length, axis=dim)
        first = lax.slice_in_dim(x, 0, width, axis=dim)
        before = lax.ppermute(last, axis, up)
        after = lax.ppermute(first, axis, down)
        x = jnp.concatenate([before, x, after], axis=dim)
    return x


def tap_sum(kernel, padded, row_count, flipped):
    tap_count = kernel.shape[0]
    running = jnp.zeros((row_count, padded.shape[1]), jnp.float32)
    for offset in range(tap_count):
        begin_row = tap_count - 1 - offset if flipped else offset
        running = running + kernel[offset][None, :] * padded[begin_row : begin_row + row_count]
    return running


def combine_stats(first_pair, second_pair):
    top_value = jnp.maximum(first_pair[0], second_pair[0])
    total_value = first_pair[1] * jnp.exp(first_pair[0] - top_value) + second_pair[1] * jnp.exp(
        second_pair[0] - top_value
    )
    return (top_value, total_value)


def row_softmax(smooth):
    local_top = jnp.max(smooth, axis=1)
    local_total = jnp.sum(jnp.exp(smooth - local_top[:, None]), axis=1)
    top_value, total_value = merged((local_top, local_total), "query", combine_stats)
    return jnp.exp(smooth - top_value[:, None]) / total_value[:, None]


def per_device(frames, queries, kernel, labels, lengths):
    frame_rows = frames[0]
    label_ids = labels[0]
    length_now = lengths[0]
    row_count = frame_rows.shape[0]
    query_count = queries.shape[0]
    width = frame_rows.shape[1]
    tap_count = kernel.shape[0]
    rim_width = tap_count // 2
    logit_scale = 10.0 / math.sqrt(width)
    frame_start = lax.axis_index("tm") * row_count
    is_valid = frame_start + jnp.arange(row_count, dtype=jnp.int32) < length_now
    query_start = lax.axis_index("query") * query_count
    query_ids = query_start + jnp.arange(query_count, dtype=jnp.int32)
    scores = (
        lax.dot_general(
            frame_rows, queries, (((1,), (1,)), ((), ())), preferred_element_type=jnp.float32
        )
        * logit_scale
    )
    scores = jnp.where(is_valid[:, None], scores, 0.0)
    wide = with_halo(scores, (("tm", 0),), 2 * rim_width)
    label_pad = with_halo(label_ids, (("tm", 0),), rim_width)
    ext_rows = row_count + 2 * rim_width
    ext_frames = frame_start - rim_width + jnp.arange(ext_rows, dtype=jnp.int32)
    ext_valid = (ext_frames >= 0) & (ext_frames < length_now)
    smooth = tap_sum(kernel, wide, ext_rows, False)
    softmax_out = row_softmax(smooth)
    positive = (label_pad[:, None] == query_ids[None, :]).astype(jnp.float32)
    grad_pad = jnp.where(ext_valid[:, None], softmax_out - positive, 0.0)
    map_grad = grad_pad[rim_width : rim_width + row_count]
    padded = wide[rim_width : rim_width + row_count + 2 * rim_width]
    score_grad = tap_sum(kernel, grad_pad, row_count, True)
    score_grad = jnp.where(is_valid[:, None], score_grad, 0.0).astype(jnp.bfloat16)
    frame_part = jnp.dot(score_grad, queries, preferred_element_type=jnp.float32)
    frame_sum = lax.psum_scatter(frame_part, "query", scatter_dimension=1, tiled=True)
    grad_frames = (frame_sum * logit_scale).astype(jnp.bfloat16)[None]
    query_part = lax.dot_general(
        score_grad, frame_rows, (((0,), (0,)), ((), ())), preferred_element_type=jnp.float32
    )
    kernel_part = jnp.stack(
        [
            jnp.sum(map_grad * padded[offset : offset + row_count], axis=0)
            for offset in range(tap_count)
        ]
    )
    query_whole, grad_kernel = lax.psum((query_part, kernel_part), ("tm", "rec"))
    col_count = width // lax.axis_size("rec")
    query_cols = lax.dynamic_slice_in_dim(
        query_whole, lax.axis_index("rec") * col_count, col_count, 1
    )
    grad_queries = (query_cols * logit_scale).astype(jnp.bfloat16)
    return (grad_frames, grad_queries, grad_kernel)


def solution(mesh):
    in_specs = (P("rec", "tm", None), P("query", None), P(None, "query"), P("rec", "tm"), P("rec"))
    out_specs = (P("rec", "tm", "query"), P("query", "rec"), P(None, "query"))
    return jax.shard_map(
        per_device, mesh=mesh, in_specs=in_specs, out_specs=out_specs, check_vma=False
    )
```

profile of v0, /device:TPU:0, one launch (start us, length us, event | category | flops | bytes accessed | tf_op | source)
XLA Modules:
  0.0 326.1 jit_solution(487026478341481205)
XLA Ops:
  8.1 0.8 slice_bitcast_fusion.1
  8.9 4.9 %collective-permute-start.2 = (s32[16]{0:T(128)S(1)}, s32[16]{0:T(128)S(1)}, u32[]{:S(2)}, u32[]{:S(2)}) collective-permute-start(s32[16]{0:T(128)S(1)} %get-tuple-element.101), channel_id=1, source_target_pairs={{0,8},{8,16},{16,24},{1,9},{9,17},{17,25},{2,10},{10,18},{18,26},{... | collective-permute-start | bytes 200 | tf_op jit(solution)/shard_map/ppermute | solution.py:26
  13.8 1.3 collective-permute-start.3
  15.8 4.6 %multiply_select_fusion = f32[512,2048]{1,0:T(8,128)S(1)} fusion(bf16[2048,1024]{1,0:T(8,128)(2,1)} %param.6, pred[512]{0:T(512)(128)(4,1)S(1)} %add_compare_fusion, bf16[1,512,1024]{2,1,0:T(8,128)(2,1)S(1)} %copy-done), kind=kOutput, calls=%fused_computation.265 | convolution fusion | flops 2149580800 | bytes 9437696 | tf_op jit(solution)/shard_map/dot_general | solution.py:71
  20.5 2.0 copy-done.3
  22.5 4.6 %collective-permute-start = (f32[32,2048]{1,0:T(8,128)S(1)}, f32[32,2048]{1,0:T(8,128)S(1)}, u32[]{:S(2)}, u32[]{:S(2)}) collective-permute-start(f32[32,2048]{1,0:T(8,128)S(1)} %get-tuple-element.66), channel_id=1, source_target_pairs={{0,8},{8,16},{16,24},{1,9},{9,17},{17,25},{2,10},{10,18},{18,26},{... | collective-permute-start | bytes 786440 | tf_op jit(solution)/shard_map/ppermute | solution.py:26
  27.0 1.3 collective-permute-start.1
  28.6 0.6 dynamic-slice
  29.9 2.1 collective-permute-done
  32.0 4.1 %collective-permute-done.1 = f32[32,2048]{1,0:T(8,128)S(1)} collective-permute-done((f32[32,2048]{1,0:T(8,128)S(1)}, f32[32,2048]{1,0:T(8,128)S(1)}, u32[]{:S(2)}, u32[]{:S(2)}) %collective-permute-start.1) | collective-permute-done | bytes 262176 | tf_op jit(solution)/shard_map/ppermute | solution.py:27
  36.1 2.8 pad_maximum_fusion.2
  38.9 22.3 %fusion.172 = (f32[544]{0:T(1024)S(1)}, f32[544,2048]{1,0:T(8,128)S(1)}) fusion(f32[32,2048]{1,0:T(8,128)S(1)} %collective-permute-done.1, f32[512,2048]{1,0:T(8,128)S(1)} %copy-done.4, f32[2048]{0:T(1024)S(1)} %bitcast.110, f32[576,2048]{1,0:T(8,128)S(1)} %pad_maximum_fusion.2, f32[2048]{0:T(1024)S(1)} %bitcast.112, f32[2048]{0:T(1024)S(1)} %bitcast.116, ...), kind=kLoop, calls=%fused_computation.285 | loop fusion | flops 75759072 | bytes 147597440 | tf_op jit(solution)/shard_map/reduce_max | solution.py:50
  61.2 2.0 copy-done.6
  63.2 0.7 exponential_reduce_fusion
  64.0 0.3 dynamic-update-slice
  64.3 0.3 dynamic-update-slice.1
  64.6 8.1 %all-reduce.3 = (f32[1088]{0:T(1024)S(1)}, f32[1088]{0:T(1024)S(1)}) all-reduce(f32[1088]{0:T(1024)S(1)} %dynamic-update-slice.1, f32[1088]{0:T(1024)S(1)} %dynamic-update-slice), channel_id=3, replica_groups=mesh['tm'=4,'query'=2,'rec'=4] {'query'}, use_global_device_ids=true, to_apply=%add.1 | all-reduce | flops 2176 | bytes 17408
  72.7 3.1 subtract_select_fusion
  75.9 18.4 %fusion.132 = bf16[512,2048]{1,0:T(8,128)(2,1)} fusion(f32[544,2048]{1,0:T(8,128)S(1)} %subtract_select_fusion, f32[2048]{0:T(1024)S(1)} %bitcast.111, f32[2048]{0:T(1024)S(1)} %bitcast.113, f32[2048]{0:T(1024)S(1)} %bitcast.117, f32[2048]{0:T(1024)S(1)} %bitcast.119, f32[2048]{0:T(1024)S(1)} %bitcast.121, f32[2048]{0:T(1024)S(1)} %bitcast.123, ...), kind=kLoop, calls=%fused_computation.201 | loop fusion | flops 70254592 | bytes 140780032 | tf_op jit(solution)/shard_map/convert_element_type | solution.py:89
  94.2 5.3 %fusion.177 = f32[512,1024]{1,0:T(8,128)} fusion(bf16[512,2048]{1,0:T(8,128)(2,1)} %fusion.132, bf16[2048,1024]{1,0:T(8,128)(2,1)S(1)} %copy-done.9), kind=kOutput, calls=%fused_computation.289 | convolution fusion | flops 2147483648 | bytes 8388608 | tf_op jit(solution)/shard_map/dot_general | solution.py:90
  99.6 0.3 all-reduce.6.cloned.1.call-start
  99.9 12.5 %fusion.129 = (f32[2048]{0:T(1024)S(1)}, f32[2048]{0:T(1024)S(1)}, f32[2048]{0:T(1024)S(1)}, f32[2048]{0:T(1024)S(1)}, f32[2048]{0:T(1024)S(1)}, /*index=5*/f32[2048]{0:T(1024)S(1)}) fusion(f32[32,2048]{1,0:T(8,128)S(1)} %collective-permute-done, f32[512,2048]{1,0:T(8,128)} %copy-done.3, f32[544,2048]{1,0:T(8,128)} %copy-done.1), kind=kLoop, calls=%fused_computation.197 | loop fusion | flops 18862080 | bytes 8699904 | tf_op jit(solution)/shard_map/reduce_sum | solution.py:98
  112.6 3.8 %fusion.78 = (f32[2048]{0:T(1024)S(1)}, f32[2048]{0:T(1024)S(1)}, f32[2048]{0:T(1024)S(1)}, f32[2048]{0:T(1024)S(1)}, f32[2048]{0:T(1024)S(1)}, /*index=5*/f32[2048]{0:T(1024)S(1)}) fusion(f32[32,2048]{1,0:T(8,128)S(1)} %collective-permute-done.1, f32[512,2048]{1,0:T(8,128)S(1)} %copy-done.5, f32[544,2048]{1,0:T(8,128)S(1)} %copy-done.2), kind=kLoop, calls=%fused_computation.146 | loop fusion | flops 18862080 | bytes 8699904 | tf_op jit(solution)/shard_map/reduce_sum | solution.py:98
  116.4 3.8 %fusion.81 = (f32[2048]{0:T(1024)S(1)}, f32[2048]{0:T(1024)S(1)}, f32[2048]{0:T(1024)S(1)}, f32[2048]{0:T(1024)S(1)}, f32[2048]{0:T(1024)S(1)}, /*index=5*/f32[2048]{0:T(1024)S(1)}) fusion(f32[32,2048]{1,0:T(8,128)S(1)} %collective-permute-done.1, f32[512,2048]{1,0:T(8,128)S(1)} %copy-done.5, f32[544,2048]{1,0:T(8,128)S(1)} %copy-done.2), kind=kLoop, calls=%fused_computation.149 | loop fusion | flops 18862080 | bytes 8699904 | tf_op jit(solution)/shard_map/reduce_sum | solution.py:98
  120.2 3.2 fusion.126
  123.4 5.4 %fusion.75 = (f32[2048]{0:T(1024)S(1)}, f32[2048]{0:T(1024)S(1)}, f32[2048]{0:T(1024)S(1)}, f32[2048]{0:T(1024)S(1)}, f32[2048]{0:T(1024)S(1)}, /*index=5*/f32[2...) fusion(f32[32,2048]{1,0:T(8,128)S(1)} %collective-permute-done.1, f32[512,2048]{1,0:T(8,128)S(1)} %copy-done.5, ...), kind=kLoop, calls=%fused_computation.143 | loop fusion | flops 27244544 | bytes 8986624 | tf_op jit(solution)/shard_map/reduce_sum | solution.py:98
  128.8 3.5 %stack.135 = f32[33,2048]{1,0:T(8,128)} concatenate(f32[1,2048]{1,0:T(1,128)S(1)} %bitcast.162, f32[1,2048]{1,0:T(1,128)S(1)} %bitcast.163, f32[1,2048]{1,0:T(1,128)S(1)} %bitcast.164, f32[1,2048]{1,0:T(1,128)S(1)} %bitcast.165, f32[1,2048]{1,0:T(1,128)S(1)} %bitcast.166, f32[1,2048]{1,0:T(1,128)S(1)} %bitcast.180, f32[1,2048]{1,0:T(1,128)S(1)} %bitcast.181, ...), dimensions={0} | concatenate | bytes 540672 | tf_op jit(solution)/shard_map/stack | solution.py:96
  132.4 7.2 %fusion.164 = f32[2048,1024]{1,0:T(8,128)} fusion(bf16[512,2048]{1,0:T(8,128)(2,1)} %fusion.132, bf16[1,512,1024]{2,1,0:T(8,128)(2,1)S(1)} %copy-done), kind=kOutput, calls=%fused_computation.267 | convolution fusion | flops 2147483648 | bytes 11534336 | tf_op jit(solution)/shard_map/dot_general | solution.py:93
  139.6 2.1 fusion.167
  141.8 172.5 %all-reduce.6.cloned.1.call-done = (f32[2048,1024]{1,0:T(8,128)}, f32[33,2048]{1,0:T(8,128)}) async-done(((f32[2048,1024]{1,0:T(8,128)}, f32[33,2048]{1,0:T(8,128)}), (f32[2048,1024]{1,0:T(8,128)}, f32[33,2048]{1,0:T(8,128)})) %all-reduce.6.cloned.1.call-update) | async-done | bytes 8658960 | tf_op jit(solution)/shard_map/psum | solution.py:102
  314.2 2.7 multiply_convert_fusion
  317.0 1.7 copy.13
  (36 shorter events, 0.8 us)
Async XLA Ops:
  8.0 7.8 %copy-start = (bf16[1,512,1024]{2,1,0:T(8,128)(2,1)S(1)}, bf16[1,512,1024]{2,1,0:T(8,128)(2,1)}, u32[]{:S(2)}) copy-start(bf16[1,512,1024]{2,1,0:T(8,128)(2,1)} %param.5) | copy-start | bytes 3145732
  8.0 131.6 %reduce-scatter.2.cloned.1.call-start = ((), (), s32[]{:S(2)}) async-start(), calls=%async_computation.1 | async-start | bytes 3145728 | tf_op jit(solution)/shard_map/reduce_scatter | solution.py:91
  8.9 21.0 %collective-permute-start.2 = (s32[16]{0:T(128)S(1)}, s32[16]{0:T(128)S(1)}, u32[]{:S(2)}, u32[]{:S(2)}) collective-permute-start(s32[16]{0:T(128)S(1)} %get-tuple-element.101), channel_id=1, source_target_pairs={{0,8},{8,16},{16,24},{1,9},{9,17},{17,25},{2,10},{10,18},{18,26},{... | collective-permute-start | bytes 200 | tf_op jit(solution)/shard_map/ppermute | solution.py:26
  13.8 16.0 %collective-permute-start.3 = (s32[16]{0:T(128)S(1)}, s32[16]{0:T(128)S(1)}, u32[]{:S(2)}, u32[]{:S(2)}) collective-permute-start(s32[16]{0:T(128)S(1)} %get-tuple-element.102), channel_id=1, source_target_pairs={{8,0},{16,8},{24,16},{9,1},{17,9},{25,17},{10,2},{18,10},{26,18},{... | collective-permute-start | bytes 200 | tf_op jit(solution)/shard_map/ppermute | solution.py:27
  15.8 12.5 %copy-start.7 = (f32[33,2048]{1,0:T(8,128)S(1)}, f32[33,2048]{1,0:T(8,128)}, u32[]{:S(2)}) copy-start(f32[33,2048]{1,0:T(8,128)} %param.7) | copy-start | bytes 811012
  15.8 12.8 %copy-start.10 = (u32[32]{0:T(128)S(1)}, u32[32]{0:T(128)}, u32[]{:S(2)}) copy-start(u32[32]{0:T(128)} %constant.48) | copy-start | bytes 388
  15.8 14.0 %copy-start.8 = (s32[1,512]{1,0:T(1,128)S(1)}, s32[1,512]{1,0:T(1,128)}, u32[]{:S(2)}) copy-start(s32[1,512]{1,0:T(1,128)} %param.8) | copy-start | bytes 6148
  20.5 2.0 copy-start.3
  22.5 9.5 %collective-permute-start = (f32[32,2048]{1,0:T(8,128)S(1)}, f32[32,2048]{1,0:T(8,128)S(1)}, u32[]{:S(2)}, u32[]{:S(2)}) collective-permute-start(f32[32,2048]{1,0:T(8,128)S(1)} %get-tuple-element.66), channel_id=1, source_target_pairs={{0,8},{8,16},{16,24},{1,9},{9,17},{17,25},{2,10},{10,18},{18,26},{... | collective-permute-start | bytes 786440 | tf_op jit(solution)/shard_map/ppermute | solution.py:26
  27.0 9.1 %collective-permute-start.1 = (f32[32,2048]{1,0:T(8,128)S(1)}, f32[32,2048]{1,0:T(8,128)S(1)}, u32[]{:S(2)}, u32[]{:S(2)}) collective-permute-start(f32[32,2048]{1,0:T(8,128)S(1)} %get-tuple-element.67), channel_id=1, source_target_pairs={{8,0},{16,8},{24,16},{9,1},{17,9},{25,17},{10,2},{18,10},{26,18},{... | collective-permute-start | bytes 786440 | tf_op jit(solution)/shard_map/ppermute | solution.py:27
  29.9 9.0 %copy-start.4 = (f32[512,2048]{1,0:T(8,128)S(1)}, f32[512,2048]{1,0:T(8,128)}, u32[]{:S(2)}) copy-start(f32[512,2048]{1,0:T(8,128)} %copy-done.3) | copy-start | bytes 12582916
  61.2 2.0 copy-start.6
  75.8 18.4 %copy-start.1 = (f32[544,2048]{1,0:T(8,128)}, f32[544,2048]{1,0:T(8,128)S(1)}, u32[]{:S(2)}) copy-start(f32[544,2048]{1,0:T(8,128)S(1)} %subtract_select_fusion) | copy-start | bytes 13369348
  75.8 18.4 %copy-start.9 = (bf16[2048,1024]{1,0:T(8,128)(2,1)S(1)}, bf16[2048,1024]{1,0:T(8,128)(2,1)}, u32[]{:S(2)}) copy-start(bf16[2048,1024]{1,0:T(8,128)(2,1)} %param.6) | copy-start | bytes 12582916
  99.6 214.7 %all-reduce.6.cloned.1.call-start = ((), (), s32[]{:S(2)}) async-start(), calls=%async_computation.2 | async-start | bytes 17432576 | tf_op jit(solution)/shard_map/psum | solution.py:102
  99.8 12.5 %copy-start.2 = (f32[544,2048]{1,0:T(8,128)S(1)}, f32[544,2048]{1,0:T(8,128)}, u32[]{:S(2)}) copy-start(f32[544,2048]{1,0:T(8,128)} %copy-done.1) | copy-start | bytes 13369348
  99.8 12.7 %copy-start.5 = (f32[512,2048]{1,0:T(8,128)S(1)}, f32[512,2048]{1,0:T(8,128)}, u32[]{:S(2)}) copy-start(f32[512,2048]{1,0:T(8,128)} %copy-done.3) | copy-start | bytes 12582916
Sparse Core Ops, SparseCore 0:
  99.7 31.1 reduce-scatter.1
Sparse Core Ops, SparseCore 1:
  139.7 174.5 all-reduce.5
where the time goes:
time: 327 us; the launch traced here: 326 us
  waiting for transfers between devices  179 us (55%)
  other arithmetic  81 us (25%)
  matrix products  17.1 us (5%)
  between operations  17.1 us (5%)
  starting transfers between devices  12.4 us (4%)
  local copies, waits for them, and re-layouts  11.7 us (4%)
  blocking collectives  8.1 us (2%)
    psum x1, waiting for transfers between devices, per_device(): lax.psum((query_part, kernel_part), ('tm', 'rec'))  172 us
    reduce_sum x5, other arithmetic, per_device(): jnp.sum(map_grad * padded[offset:offset + row_count], axis=0)  28.7 us
    reduce_max x1, other arithmetic, row_softmax(): local_top = jnp.max(smooth, axis=1)  22.3 us
    convert_element_type x1, other arithmetic, per_device(): jnp.where(is_valid[:, None], score_grad, 0.0).astype(jnp.bfloat16)  18.4 us
    ppermute x2, starting transfers between devices, with_halo(): before = lax.ppermute(last, axis, up)  9.51 us
    unnamed x1, blocking collectives  8.1 us
    dot_general x1, matrix products, per_device(): lax.dot_general(score_grad, frame_rows, (((0,), (0,)), ((), ())), preferr...  7.19 us
    unnamed x28, local copies, waits for them, and re-layouts  7.14 us
  transfers between devices with their start and end apart: 6, of which 3 were waited for; matrix products, arithmetic and copies ran while one was open for 14% of the time, Pallas kernels for 0%

commit v1 on v0

--- a/solution.py
+++ b/solution.py
@@ -7,26 +7,22 @@
 
 
 def merged(x, axis, combine):
-    everything = jax.tree.map(lambda part: lax.all_gather(part, axis), x)
-    first = jax.tree.map(lambda part: part[0], everything)
-
-    def step(k, so_far):
-        return combine(so_far, jax.tree.map(lambda part: part[k], everything))
-
-    return lax.fori_loop(1, lax.axis_size(axis), step, first)
+    peers = lax.axis_size(axis)
+    step = 1
+    while step < peers:
+        swap = [(i, i ^ step) for i in range(peers)]
+        x = combine(x, lax.ppermute(x, axis, swap))
+        step *= 2
+    return x
 
 
-def with_halo(x, sides, width):
-    for axis, dim in sides:
-        peers, length = (lax.axis_size(axis), x.shape[dim])
-        up = [(i, (i + 1) % peers) for i in range(peers - 1)]
-        down = [(j, i) for i, j in up]
-        last = lax.slice_in_dim(x, length - width, length, axis=dim)
-        first = lax.slice_in_dim(x, 0, width, axis=dim)
-        before = lax.ppermute(last, axis, up)
-        after = lax.ppermute(first, axis, down)
-        x = jnp.concatenate([before, x, after], axis=dim)
-    return x
+def halo_rows(x, axis, width):
+    peers = lax.axis_size(axis)
+    up = [(i, i + 1) for i in range(peers - 1)]
+    down = [(i + 1, i) for i in range(peers - 1)]
+    before = lax.ppermute(x[x.shape[0] - width :], axis, up)
+    after = lax.ppermute(x[:width], axis, down)
+    return lax.optimization_barrier((before, after))
 
 
 def tap_sum(kernel, padded, row_count, flipped):
@@ -43,13 +39,14 @@
     total_value = first_pair[1] * jnp.exp(first_pair[0] - top_value) + second_pair[1] * jnp.exp(
         second_pair[0] - top_value
     )
-    return (top_value, total_value)
+    return jnp.stack([top_value, total_value])
 
 
 def row_softmax(smooth):
     local_top = jnp.max(smooth, axis=1)
     local_total = jnp.sum(jnp.exp(smooth - local_top[:, None]), axis=1)
-    top_value, total_value = merged((local_top, local_total), "query", combine_stats)
+    stats = merged(jnp.stack([local_top, local_total]), "query", combine_stats)
+    top_value, total_value = stats[0], stats[1]
     return jnp.exp(smooth - top_value[:, None]) / total_value[:, None]
 
 
@@ -67,15 +64,38 @@
     is_valid = frame_start + jnp.arange(row_count, dtype=jnp.int32) < length_now
     query_start = lax.axis_index("query") * query_count
     query_ids = query_start + jnp.arange(query_count, dtype=jnp.int32)
-    scores = (
-        lax.dot_general(
-            frame_rows, queries, (((1,), (1,)), ((), ())), preferred_element_type=jnp.float32
+    halo = 2 * rim_width
+    tagged = jnp.concatenate(
+        [
+            frame_rows.astype(jnp.float32),
+            jnp.broadcast_to(label_ids.astype(jnp.float32)[:, None], (row_count, 128)),
+        ],
+        axis=1,
+    )
+    before, after = halo_rows(tagged, "tm", halo)
+    rim_rows = jnp.concatenate([before[:, :width], after[:, :width]]).astype(jnp.bfloat16)
+
+    def scored(rows):
+        return (
+            lax.dot_general(
+                rows, queries, (((1,), (1,)), ((), ())), preferred_element_type=jnp.float32
+            )
+            * logit_scale
         )
-        * logit_scale
+
+    inner = scored(frame_rows)
+    rim = scored(rim_rows)
+    wide = jnp.concatenate([rim[:halo], inner, rim[halo:]])
+    wide_frames = frame_start - halo + jnp.arange(row_count + 2 * halo, dtype=jnp.int32)
+    wide_valid = (wide_frames >= 0) & (wide_frames < length_now)
+    wide = jnp.where(wide_valid[:, None], wide, 0.0)
+    label_pad = jnp.concatenate(
+        [
+            before[halo - rim_width :, width].astype(jnp.int32),
+            label_ids,
+            after[:rim_width, width].astype(jnp.int32),
+        ]
     )
-    scores = jnp.where(is_valid[:, None], scores, 0.0)
-    wide = with_halo(scores, (("tm", 0),), 2 * rim_width)
-    label_pad = with_halo(label_ids, (("tm", 0),), rim_width)
     ext_rows = row_count + 2 * rim_width
     ext_frames = frame_start - rim_width + jnp.arange(ext_rows, dtype=jnp.int32)
     ext_valid = (ext_frames >= 0) & (ext_frames < length_now)
@@ -99,11 +119,8 @@
             for offset in range(tap_count)
         ]
     )
-    query_whole, grad_kernel = lax.psum((query_part, kernel_part), ("tm", "rec"))
-    col_count = width // lax.axis_size("rec")
-    query_cols = lax.dynamic_slice_in_dim(
-        query_whole, lax.axis_index("rec") * col_count, col_count, 1
-    )
+    query_cols = lax.psum_scatter(query_part, "rec", scatter_dimension=1, tiled=True)
+    query_cols, grad_kernel = lax.psum((query_cols, lax.psum(kernel_part, "rec")), "tm")
     grad_queries = (query_cols * logit_scale).astype(jnp.bfloat16)
     return (grad_frames, grad_queries, grad_kernel)
 

time: 327 us -> 355 us (1.086)
  waiting for transfers between devices: 179 us -> 227 us
  other arithmetic: 81 us -> 70.2 us
  blocking collectives: 8.1 us -> 0 us
  matrix products: 17.1 us -> 22.9 us
    reduce_scatter x0 -> x1, waiting for transfers between devices: none -> 73.9 us  [per_device(): lax.psum_scatter(query_part, 'rec', scatter_dimension=1, tiled=True)]
    psum x1 -> x2, waiting for transfers between devices: 172 us -> 118 us  [the longest x1 97.2 us: per_device(): lax.psum((query_cols, lax.psum(kernel_part, 'rec')), 'tm')]
    reduce_scatter x1, waiting for transfers between devices: 0.02 us -> 34.2 us  [per_device(): lax.psum_scatter(frame_part, 'query', scatter_dimension=1, tiled=True)]
    reduce_sum x5 -> x3, other arithmetic: 28.7 us -> 20 us  [per_device(): jnp.sum(map_grad * padded[offset:offset + row_count], axis=0)]
    unnamed x1 -> x0, blocking collectives: 8.1 us -> none
    dot_general x1 -> x2, matrix products: 4.6 us -> 10.2 us  [scored(): lax.dot_general(rows, queries, (((1,), (1,)), ((), ())), preferred_elemen...]
    unnamed x28 -> x37, local copies, waits for them, and re-layouts: 7.14 us -> 1.8 us
    ppermute x4 -> x3, waiting for transfers between devices: 6.19 us -> 1.58 us  [the longest x1 1.58 us: merged(): x = combine(x, lax.ppermute(x, axis, swap))]
  transfers between devices with their start and end apart: 6 -> 7, of which waited for: 3 -> 5; matrix products, arithmetic and copies ran while one was open for 14% -> 6% of each run, Pallas kernels for 0% -> 0%
where the time goes in v1:
time: 355 us; the launch traced here: 354 us
  waiting for transfers between devices  227 us (64%)
  other arithmetic  70.2 us (20%)
  matrix products  22.9 us (6%)
  between operations  14.8 us (4%)
  local copies, waits for them, and re-layouts  9.67 us (3%)
  starting transfers between devices  9.07 us (3%)
    psum x1, waiting for transfers between devices, per_device(): lax.psum((query_cols, lax.psum(kernel_part, 'rec')), 'tm')  97.2 us
    reduce_scatter x1, waiting for transfers between devices, per_device(): lax.psum_scatter(query_part, 'rec', scatter_dimension=1, tiled=True)  73.9 us
    reduce_scatter x1, waiting for transfers between devices, per_device(): lax.psum_scatter(frame_part, 'query', scatter_dimension=1, tiled=True)  34.2 us
    reduce_max x1, other arithmetic, row_softmax(): local_top = jnp.max(smooth, axis=1)  22.3 us
    psum x1, waiting for transfers between devices, per_device(): lax.psum(kernel_part, 'rec')  20.5 us
    reduce_sum x3, other arithmetic, per_device(): jnp.sum(map_grad * padded[offset:offset + row_count], axis=0)  20 us
    convert_element_type x1, other arithmetic, per_device(): jnp.where(is_valid[:, None], score_grad, 0.0).astype(jnp.bfloat16)  17.9 us
    dot_general x2, matrix products, scored(): lax.dot_general(rows, queries, (((1,), (1,)), ((), ())), preferred_elemen...  10.2 us
  transfers between devices with their start and end apart: 7, of which 5 were waited for; matrix products, arithmetic and copies ran while one was open for 6% of the time, Pallas kernels for 0%

profile of v1, /device:TPU:0, one launch (start us, length us, event | category | flops | bytes accessed | tf_op | source)
XLA Modules:
  0.0 354.0 jit_solution(133784667908076871)
XLA Ops:
  7.2 0.8 convert_element_type.36
  8.0 1.5 bitcast_convert_fusion
  9.5 0.1 broadcast_in_dim.54
  9.7 1.3 collective-permute-start.1
  11.0 5.6 %collective-permute-start = (f32[32,1152]{1,0:T(8,128)S(1)}, f32[32,1152]{1,0:T(8,128)S(1)}, u32[]{:S(2)}, u32[]{:S(2)}) collective-permute-start(f32[32,1152]{1,0:T(8,128)S(1)} %get-tuple-element.55), channel_id=1, source_target_pairs={{0,8},{8,16},{16,24},{1,9},{9,17},{17,25},{2,10},{10,18},{18,26},{... | collective-permute-start | bytes 442376 | tf_op jit(solution)/shard_map/ppermute | solution.py:23
  16.6 0.1 fusion.117
  16.7 0.1 fusion.116
  17.5 6.5 %convolution_multiply_fusion = f32[512,2048]{1,0:T(8,128)} fusion(bf16[2048,1024]{1,0:T(8,128)(2,1)} %param.6, bf16[1,512,1024]{2,1,0:T(8,128)(2,1)S(1)} %copy-done.1), kind=kOutput, calls=%fused_computation.200 | convolution fusion | flops 2148532224 | bytes 9437184 | tf_op jit(solution)/shard_map/dot_general | solution.py:80
  24.1 0.1 convert_reduce_fusion
  24.2 3.7 %convolution_multiply_fusion.1 = f32[64,2048]{1,0:T(8,128)S(1)} fusion(bf16[2048,1024]{1,0:T(8,128)(2,1)} %param.6, bf16[32,1024]{1,0:T(8,128)(2,1)S(1)} %slice.1206, bf16[32,1024]{1,0:T(8,128)(2,1)S(1)} %slice.1207), kind=kOutput, calls=%fused_computation.201 | convolution fusion | flops 268828672 | bytes 4849664 | tf_op jit(solution)/shard_map/dot_general | solution.py:80
  28.0 0.4 maximum_select_fusion
  28.5 22.3 %fusion.113 = (f32[544]{0:T(1024)S(1)}, f32[544,2048]{1,0:T(8,128)S(1)}) fusion(f32[576,2048]{1,0:T(8,128)S(1)} %maximum_select_fusion, f32[2048]{0:T(1024)S(1)} %bitcast.108, f32[2048]{0:T(1024)S(1)} %bitcast.110, f32[2048]{0:T(1024)S(1)} %bitcast.114, f32[2048]{0:T(1024)S(1)} %bitcast.116, f32[2048]{0:T(1024)S(1)} %bitcast.118, f32[2048]{0:T(1024)S(1)} %bitcast.120, ...), kind=kLoop, calls=%fused_computation.234 | loop fusion | flops 73530848 | bytes 151791744 | tf_op jit(solution)/shard_map/reduce_max | solution.py:46
  50.8 0.7 exponential_reduce_fusion
  51.6 2.0 collective-permute-start.2
  53.6 0.1 pad_add_fusion
  53.7 1.6 collective-permute-done.2
  55.3 1.5 subtract_select_fusion
  56.8 5.9 %fusion.49 = (f32[2048]{0:T(1024)}, f32[2048]{0:T(1024)}, f32[2048]{0:T(1024)}, f32[2048]{0:T(1024)}, f32[2048]{0:T(1024)}, /*index=5*/f32[2048]{0:T(1024)}, f32[2048]{0:T(1024)}, f32[2048]{0:T(1024)}, f32[2048]{0:T(1024)}) fusion(f32[576,2048]{1,0:T(8,128)S(1)} %maximum_select_fusion, f32[544,2048]{1,0:T(8,128)S(1)} %subtract_select_fusion), kind=kLoop, calls=%fused_computation.103 | loop fusion | flops 18855936 | bytes 42016768 | tf_op jit(solution)/shard_map/reduce_sum | solution.py:118
  62.7 5.6 %fusion.32 = (f32[2048]{0:T(1024)}, f32[2048]{0:T(1024)}, f32[2048]{0:T(1024)}, f32[2048]{0:T(1024)}, f32[2048]{0:T(1024)}, /*index=5*/f32[2048]{0:T(1024)}, f32[2048]{0:T(1024)}, f32[2048]{0:T(1024)}, f32[2048]{0:T(1024)}) fusion(f32[576,2048]{1,0:T(8,128)S(1)} %maximum_select_fusion, f32[544,2048]{1,0:T(8,128)S(1)} %subtract_select_fusion), kind=kLoop, calls=%fused_computation.69 | loop fusion | flops 18855936 | bytes 42016768 | tf_op jit(solution)/shard_map/reduce_sum | solution.py:118
  68.3 8.5 %fusion.40 = (f32[2048]{0:T(1024)}, f32[2048]{0:T(1024)}, f32[2048]{0:T(1024)}, f32[2048]{0:T(1024)}, f32[2048]{0:T(1024)}, /*index=5*/f32[2048]{0:T(1024)}, f32...) fusion(f32[576,2048]{1,0:T(8,128)S(1)} %maximum_select_fusion, ...), kind=kLoop, calls=%fused_computation.85 | loop fusion | flops 31426560 | bytes 67231744 | tf_op jit(solution)/shard_map/reduce_sum | solution.py:118
  76.9 17.9 %fusion.67 = bf16[512,2048]{1,0:T(8,128)(2,1)S(1)} fusion(f32[544,2048]{1,0:T(8,128)S(1)} %subtract_select_fusion, f32[2048]{0:T(1024)S(1)} %bitcast.109, f32[2048]{0:T(1024)S(1)} %bitcast.111, f32[2048]{0:T(1024)S(1)} %bitcast.115, f32[2048]{0:T(1024)S(1)} %bitcast.117, f32[2048]{0:T(1024)S(1)} %bitcast.119, f32[2048]{0:T(1024)S(1)} %bitcast.121, ...), kind=kLoop, calls=%fused_computation.137 | loop fusion | flops 70254592 | bytes 140780032 | tf_op jit(solution)/shard_map/convert_element_type | solution.py:109
  94.8 7.5 %stack.147 = f32[33,2048]{1,0:T(8,128)} concatenate(f32[1,2048]{1,0:T(1,128)} %bitcast.160, f32[1,2048]{1,0:T(1,128)} %bitcast.177, f32[1,2048]{1,0:T(1,128)} %bitcast.178, f32[1,2048]{1,0:T(1,128)} %bitcast.179, f32[1,2048]{1,0:T(1,128)} %bitcast.180, f32[1,2048]{1,0:T(1,128)} %bitcast.181, f32[1,2048]{1,0:T(1,128)} %bitcast.182, f32[1,2048]{1,0:T(1,128)} %bitcast.158, ...), dimensions={0} | concatenate | bytes 540672 | tf_op jit(solution)/shard_map/stack | solution.py:116
  102.3 6.8 %fusion.99 = f32[2048,1024]{1,0:T(8,128)} fusion(bf16[512,2048]{1,0:T(8,128)(2,1)S(1)} %fusion.67, bf16[1,512,1024]{2,1,0:T(8,128)(2,1)} %param.5), kind=kOutput, calls=%fused_computation.203 | convolution fusion | flops 2147483648 | bytes 11534336 | tf_op jit(solution)/shard_map/dot_general | solution.py:113
  109.2 5.8 %fusion.118 = f32[512,1024]{1,0:T(8,128)} fusion(bf16[512,2048]{1,0:T(8,128)(2,1)S(1)} %fusion.67, bf16[2048,1024]{1,0:T(8,128)(2,1)} %param.6), kind=kOutput, calls=%fused_computation.238 | convolution fusion | flops 2147483648 | bytes 8388608 | tf_op jit(solution)/shard_map/dot_general | solution.py:110
  115.1 0.0 all-reduce.6.cloned.1.call-start
  115.2 20.5 %all-reduce.4.cloned.1.call-done = f32[33,2048]{1,0:T(8,128)} async-done(((f32[33,2048]{1,0:T(8,128)}), f32[33,2048]{1,0:T(8,128)}) %all-reduce.4.cloned.1.call-update) | async-done | bytes 270352 | tf_op jit(solution)/shard_map/psum | solution.py:123
  135.6 73.9 %reduce-scatter.5.cloned.1.call-done = f32[2048,256]{1,0:T(8,128)} async-done(((f32[2048,1024]{1,0:T(8,128)}), f32[2048,256]{1,0:T(8,128)}) %reduce-scatter.5.cloned.1.call-update) | async-done | bytes 2097168 | tf_op jit(solution)/shard_map/reduce_scatter | solution.py:122
  209.5 34.2 %reduce-scatter.3.cloned.1.call-done = f32[512,512]{1,0:T(8,128)} async-done(((f32[512,1024]{1,0:T(8,128)}), f32[512,512]{1,0:T(8,128)}) %reduce-scatter.3.cloned.1.call-update) | async-done | bytes 1048592 | tf_op jit(solution)/shard_map/reduce_scatter | solution.py:111
  243.7 2.1 fusion.102
  245.8 97.2 %all-reduce.6.cloned.1.call-done = (f32[2048,256]{1,0:T(8,128)}, f32[33,2048]{1,0:T(8,128)}) async-done(((f32[2048,256]{1,0:T(8,128)}, f32[33,2048]{1,0:T(8,128)}), (f32[2048,256]{1,0:T(8,128)}, f32[33,2048]{1,0:T(8,128)})) %all-reduce.6.cloned.1.call-update) | async-done | bytes 2367504 | tf_op jit(solution)/shard_map/psum | solution.py:123
  343.0 2.7 multiply_convert_fusion
  345.8 1.7 copy.12
  (58 shorter events, 0.4 us)
Async XLA Ops:
  7.2 10.4 %copy-start.1 = (bf16[1,512,1024]{2,1,0:T(8,128)(2,1)S(1)}, bf16[1,512,1024]{2,1,0:T(8,128)(2,1)}, u32[]{:S(2)}) copy-start(bf16[1,512,1024]{2,1,0:T(8,128)(2,1)} %param.5) | copy-start | bytes 3145732
  7.2 9.4 %copy-start.2 = (f32[33,2048]{1,0:T(8,128)S(1)}, f32[33,2048]{1,0:T(8,128)}, u32[]{:S(2)}) copy-start(f32[33,2048]{1,0:T(8,128)} %param.7) | copy-start | bytes 811012
  7.2 128.4 %all-reduce.4.cloned.1.call-start = ((), (), s32[]{:S(2)}) async-start(), calls=%async_computation.4 | async-start | bytes 655360 | tf_op jit(solution)/shard_map/psum | solution.py:123
  9.7 14.4 %collective-permute-start.1 = (f32[32,1152]{1,0:T(8,128)S(1)}, f32[32,1152]{1,0:T(8,128)S(1)}, u32[]{:S(2)}, u32[]{:S(2)}) collective-permute-start(f32[32,1152]{1,0:T(8,128)S(1)} %get-tuple-element.54), channel_id=1, source_target_pairs={{8,0},{16,8},{24,16},{9,1},{17,9},{25,17},{10,2},{18,10},{26,18},{... | collective-permute-start | bytes 442376 | tf_op jit(solution)/shard_map/ppermute | solution.py:24
  11.0 13.1 %collective-permute-start = (f32[32,1152]{1,0:T(8,128)S(1)}, f32[32,1152]{1,0:T(8,128)S(1)}, u32[]{:S(2)}, u32[]{:S(2)}) collective-permute-start(f32[32,1152]{1,0:T(8,128)S(1)} %get-tuple-element.55), channel_id=1, source_target_pairs={{0,8},{8,16},{16,24},{1,9},{9,17},{17,25},{2,10},{10,18},{18,26},{... | collective-permute-start | bytes 442376 | tf_op jit(solution)/shard_map/ppermute | solution.py:23
  16.8 11.6 %copy-start.3 = (f32[1,2048]{1,0:T(1,128)}, f32[1,2048]{1,0:T(1,128)S(1)}, u32[]{:S(2)}) copy-start(f32[1,2048]{1,0:T(1,128)S(1)} %get-tuple-element.70) | copy-start | bytes 24580
  16.8 11.6 %copy-start.5 = (f32[1,2048]{1,0:T(1,128)}, f32[1,2048]{1,0:T(1,128)S(1)}, u32[]{:S(2)}) copy-start(f32[1,2048]{1,0:T(1,128)S(1)} %get-tuple-element.71) | copy-start | bytes 24580
  16.8 11.6 %copy-start.7 = (f32[1,2048]{1,0:T(1,128)}, f32[1,2048]{1,0:T(1,128)S(1)}, u32[]{:S(2)}) copy-start(f32[1,2048]{1,0:T(1,128)S(1)} %get-tuple-element.72) | copy-start | bytes 24580
  16.8 11.6 %copy-start.9 = (f32[1,2048]{1,0:T(1,128)}, f32[1,2048]{1,0:T(1,128)S(1)}, u32[]{:S(2)}) copy-start(f32[1,2048]{1,0:T(1,128)S(1)} %get-tuple-element.73) | copy-start | bytes 24580
  16.8 11.6 %copy-start.11 = (f32[1,2048]{1,0:T(1,128)}, f32[1,2048]{1,0:T(1,128)S(1)}, u32[]{:S(2)}) copy-start(f32[1,2048]{1,0:T(1,128)S(1)} %get-tuple-element.74) | copy-start | bytes 24580
  16.9 11.6 %copy-start.13 = (f32[1,2048]{1,0:T(1,128)}, f32[1,2048]{1,0:T(1,128)S(1)}, u32[]{:S(2)}) copy-start(f32[1,2048]{1,0:T(1,128)S(1)} %get-tuple-element.75) | copy-start | bytes 24580
  16.9 11.6 %copy-start.15 = (f32[1,2048]{1,0:T(1,128)}, f32[1,2048]{1,0:T(1,128)S(1)}, u32[]{:S(2)}) copy-start(f32[1,2048]{1,0:T(1,128)S(1)} %get-tuple-element.76) | copy-start | bytes 24580
  24.1 4.0 %copy-start = (f32[512,2048]{1,0:T(8,128)S(1)}, f32[512,2048]{1,0:T(8,128)}, u32[]{:S(2)}) copy-start(f32[512,2048]{1,0:T(8,128)} %convolution_multiply_fusion) | copy-start | bytes 12582916
  50.8 2.8 copy-start.17
  51.6 3.7 %collective-permute-start.2 = (f32[2,544]{1,0:T(2,128)S(1)}, f32[2,544]{1,0:T(2,128)S(1)}, u32[]{:S(2)}, u32[]{:S(2)}) collective-permute-start(f32[2,544]{1,0:T(2,128)S(1)} %pad_maximum_fusion.2), channel_id=1, source_target_pairs={{0,4},{4,0},{1,5},{5,1},{2,6},{6,2},{3,7},{7,3},{8,12},{12,8},{9,1... | collective-permute-start | bytes 13064 | tf_op jit(solution)/shard_map/ppermute | solution.py:14
  68.3 8.6 %copy-start.4 = (f32[1,2048]{1,0:T(1,128)S(1)}, f32[1,2048]{1,0:T(1,128)}, u32[]{:S(2)}) copy-start(f32[1,2048]{1,0:T(1,128)} %copy-done.3) | copy-start | bytes 24580
  68.3 8.6 %copy-start.6 = (f32[1,2048]{1,0:T(1,128)S(1)}, f32[1,2048]{1,0:T(1,128)}, u32[]{:S(2)}) copy-start(f32[1,2048]{1,0:T(1,128)} %copy-done.5) | copy-start | bytes 24580
  68.3 8.6 %copy-start.8 = (f32[1,2048]{1,0:T(1,128)S(1)}, f32[1,2048]{1,0:T(1,128)}, u32[]{:S(2)}) copy-start(f32[1,2048]{1,0:T(1,128)} %copy-done.7) | copy-start | bytes 24580
  68.3 8.6 %copy-start.10 = (f32[1,2048]{1,0:T(1,128)S(1)}, f32[1,2048]{1,0:T(1,128)}, u32[]{:S(2)}) copy-start(f32[1,2048]{1,0:T(1,128)} %copy-done.9) | copy-start | bytes 24580
  68.3 8.6 %copy-start.12 = (f32[1,2048]{1,0:T(1,128)S(1)}, f32[1,2048]{1,0:T(1,128)}, u32[]{:S(2)}) copy-start(f32[1,2048]{1,0:T(1,128)} %copy-done.11) | copy-start | bytes 24580
  68.3 8.6 %copy-start.14 = (f32[1,2048]{1,0:T(1,128)S(1)}, f32[1,2048]{1,0:T(1,128)}, u32[]{:S(2)}) copy-start(f32[1,2048]{1,0:T(1,128)} %copy-done.13) | copy-start | bytes 24580
  68.3 8.6 %copy-start.16 = (f32[1,2048]{1,0:T(1,128)S(1)}, f32[1,2048]{1,0:T(1,128)}, u32[]{:S(2)}) copy-start(f32[1,2048]{1,0:T(1,128)} %copy-done.15) | copy-start | bytes 24580
  102.3 107.2 %reduce-scatter.5.cloned.1.call-start = ((), (), s32[]{:S(2)}) async-start(), calls=%async_computation.3 | async-start | bytes 10485760 | tf_op jit(solution)/shard_map/reduce_scatter | solution.py:122
  109.2 134.5 %reduce-scatter.3.cloned.1.call-start = ((), (), s32[]{:S(2)}) async-start(), calls=%async_computation.2 | async-start | bytes 3145728 | tf_op jit(solution)/shard_map/reduce_scatter | solution.py:111
  115.1 227.9 %all-reduce.6.cloned.1.call-start = ((), (), s32[]{:S(2)}) async-start(), calls=%async_computation.5 | async-start | bytes 4849664 | tf_op jit(solution)/shard_map/psum | solution.py:123
Sparse Core Ops, SparseCore 0:
  102.4 33.2 all-reduce.3
  138.2 71.2 reduce-scatter.4
  211.8 31.8 reduce-scatter.2
  246.0 97.0 all-reduce.5

commit v2 on v1

--- a/solution.py
+++ b/solution.py
@@ -1,8 +1,11 @@
+import functools
 import math
 
 import jax
 import jax.numpy as jnp
 from jax import lax
+from jax.experimental import pallas as pl
+from jax.experimental.pallas import tpu as pltpu
 from jax.sharding import PartitionSpec as P
 
 
@@ -23,6 +26,279 @@
     before = lax.ppermute(x[x.shape[0] - width :], axis, up)
     after = lax.ppermute(x[:width], axis, down)
     return lax.optimization_barrier((before, after))
+
+
+MESH = pl.DeviceIdType.MESH
+
+
+def bit_reversed(p, bits):
+    return sum(((p >> k) & 1) << (bits - 1 - k) for k in range(bits))
+
+
+def gradient_kernel(
+    dims, scale, sg_ref, fr_ref, qu_ref, kp_ref, gf_ref, gq_ref, gk_ref, *scratch
+):
+    tms, peers, recs, chunk = dims
+    bits = recs.bit_length() - 1
+    acc, scratch = scratch[:bits], scratch[bits:]
+    arrived, scratch = scratch[:bits], scratch[bits:]
+    kacc, scratch = scratch[:bits], scratch[bits:]
+    karrived, scratch = scratch[:bits], scratch[bits:]
+    (mid, outer, inner, kmid, kouter, kinner, fpart, fin) = scratch[:8]
+    (rec_send, rec_recv, in_send, out_recv, out_send, inn_recv, f_send, f_recv) = scratch[8:]
+
+    t = lax.axis_index("tm")
+    y = lax.axis_index("query")
+    r = lax.axis_index("rec")
+    half = tms // 2
+    low = t < half
+    is_end = (t == 0) | (t == tms - 1)
+    is_mid = (t == half - 1) | (t == half)
+    inward = jnp.where(low, t + 1, t - 1)
+    outward = jnp.where(low, lax.rem(t + tms - 1, tms), lax.rem(t + 1, tms))
+    my_bits = [lax.rem(r // (1 << k), 2) for k in range(bits)]
+    rec_peers = [r + (1 - 2 * my_bits[k]) * (1 << k) for k in range(bits)]
+
+    barrier = pltpu.get_barrier_semaphore()
+
+    def greet(device):
+        pl.semaphore_signal(barrier, inc=1, device_id=device, device_id_type=MESH)
+
+    for peer in rec_peers:
+        greet({"rec": peer})
+    for d in range(1, peers):
+        greet({"query": lax.rem(y + d, peers)})
+    greet({"tm": inward})
+
+    @pl.when(jnp.logical_not(is_end))
+    def _():
+        greet({"tm": outward})
+
+    pl.semaphore_wait(barrier, jnp.where(is_end, bits + peers, bits + peers + 1))
+
+    queries, width = (qu_ref.shape[0], fr_ref.shape[1])
+    count = queries // chunk
+    cols = width // recs
+    fcols = width // peers
+    row_count = sg_ref.shape[0]
+
+    def copy(src, dst, send, recv, device):
+        return pltpu.make_async_remote_copy(
+            src_ref=src,
+            dst_ref=dst,
+            send_sem=send,
+            recv_sem=recv,
+            device_id=device,
+            device_id_type=MESH,
+        )
+
+    def at(c):
+        return pl.ds(pl.multiple_of(c * chunk, chunk), chunk)
+
+    def f_copy(d):
+        p = lax.rem(y + d, peers)
+        return copy(fpart.at[p], fin.at[d - 1], f_send.at[d - 1], f_recv.at[d - 1], {"query": p})
+
+    def f_compute(p):
+        tile = 128
+        columns = pl.ds(pl.multiple_of(p * fcols, fcols), fcols)
+
+        def body(i, carry):
+            rows = pl.ds(pl.multiple_of(i * tile, tile), tile)
+            fpart[p, rows, :] = jnp.dot(
+                sg_ref[rows, :], qu_ref[:, columns], preferred_element_type=jnp.float32
+            )
+            return carry
+
+        lax.fori_loop(0, row_count // tile, body, 0)
+
+    def rec_copies(k, c):
+        n = recs >> k
+        theirs = (1 - my_bits[k]) * (n // 2)
+        device = {"rec": rec_peers[k]}
+        return (
+            copy(
+                acc[k].at[pl.ds(theirs, n // 2), at(c)],
+                arrived[k].at[:, at(c)],
+                rec_send.at[k, 0, c],
+                rec_recv.at[k, 0, c],
+                device,
+            ),
+            copy(
+                kacc[k].at[c],
+                karrived[k].at[c],
+                rec_send.at[k, 1, c],
+                rec_recv.at[k, 1, c],
+                device,
+            ),
+        )
+
+    def summed(k, c):
+        for one in rec_copies(k, c):
+            one.wait_recv()
+        n = recs >> k
+        mine = my_bits[k] * (n // 2)
+        total = acc[k][pl.ds(mine, n // 2), at(c), :] + arrived[k][:, at(c), :]
+        return total, kacc[k][c] + karrived[k][c]
+
+    def inward_copies(c, to_mid):
+        big, small = (inner, kinner) if to_mid else (outer, kouter)
+        recv = inn_recv if to_mid else out_recv
+        device = {"tm": inward}
+        return (
+            copy(mid.at[at(c)], big.at[at(c)], in_send.at[0, c], recv.at[0, c], device),
+            copy(kmid.at[c], small.at[c], in_send.at[1, c], recv.at[1, c], device),
+        )
+
+    def outward_copies(c):
+        device = {"tm": outward}
+        return (
+            copy(inner.at[at(c)], inner.at[at(c)], out_send.at[0, c], inn_recv.at[0, c], device),
+            copy(kinner.at[c], kinner.at[c], out_send.at[1, c], inn_recv.at[1, c], device),
+        )
+
+    def start(c):
+        part = lax.dot_general(
+            sg_ref[:, at(c)],
+            fr_ref[...],
+            (((0,), (0,)), ((), ())),
+            preferred_element_type=jnp.float32,
+        )
+        for p in range(recs):
+            j = bit_reversed(p, bits)
+            acc[0][p, at(c), :] = part[:, j * cols : (j + 1) * cols]
+        kacc[0][c] = kp_ref[:, at(c)]
+        for one in rec_copies(0, c):
+            one.start()
+
+    def exchange(k, c):
+        total, ktotal = summed(k - 1, c)
+        acc[k][:, at(c), :] = total
+        kacc[k][c] = ktotal
+        for one in rec_copies(k, c):
+            one.start()
+
+    def gather_in(c):
+        total, ktotal = summed(bits - 1, c)
+        mid[at(c), :] = total[0]
+        kmid[c] = ktotal
+
+        @pl.when(jnp.logical_not(is_end))
+        def _():
+            for one in inward_copies(c, False):
+                one.wait_recv()
+            mid[at(c), :] += outer[at(c), :]
+            kmid[c] += kouter[c]
+
+        @pl.when(is_mid)
+        def _():
+            for one in inward_copies(c, True):
+                one.start()
+
+        @pl.when(jnp.logical_not(is_mid))
+        def _():
+            for one in inward_copies(c, False):
+                one.start()
+
+    def spread_out(c):
+        for one in inward_copies(c, True):
+            one.wait_recv()
+
+        @pl.when(is_mid)
+        def _():
+            inner[at(c), :] += mid[at(c), :]
+            kinner[c] += kmid[c]
+
+        @pl.when(jnp.logical_not(is_end))
+        def _():
+            for one in outward_copies(c):
+                one.start()
+
+        gq_ref[at(c), :] = (inner[at(c), :] * scale).astype(gq_ref.dtype)
+        gk_ref[:, at(c)] = kinner[c]
+
+    for d in range(1, peers):
+        f_compute(lax.rem(y + d, peers))
+        f_copy(d).start()
+
+    lag = bits + 4
+    stages = [(0, start)]
+    stages += [(k, functools.partial(exchange, k)) for k in range(1, bits)]
+    stages += [(bits, gather_in), (lag, spread_out)]
+
+    def step(s, carry):
+        for delay, stage in stages:
+            @pl.when((s >= delay) & (s < count + delay))
+            def _(stage=stage, delay=delay):
+                stage(s - delay)
+        return carry
+
+    lax.fori_loop(0, count + lag, step, 0)
+
+    f_compute(y)
+    for d in range(1, peers):
+        f_copy(d).wait_recv()
+    total = fpart[y]
+    for d in range(1, peers):
+        total = total + fin[d - 1]
+    gf_ref[...] = (total * scale).astype(gf_ref.dtype)
+    for d in range(1, peers):
+        f_copy(d).wait_send()
+
+    def drain(c, carry):
+        for k in range(bits):
+            for one in rec_copies(k, c):
+                one.wait_send()
+        for one in inward_copies(c, False):
+            one.wait_send()
+
+        @pl.when(jnp.logical_not(is_end))
+        def _():
+            for one in outward_copies(c):
+                one.wait_send()
+
+        return carry
+
+    lax.fori_loop(0, count, drain, 0)
+
+
+def gradients(score_grad, frame_rows, queries, kernel_part, scale):
+    tms, peers, recs = (lax.axis_size("tm"), lax.axis_size("query"), lax.axis_size("rec"))
+    bits = recs.bit_length() - 1
+    row_count, width = frame_rows.shape
+    query_count = queries.shape[0]
+    taps = kernel_part.shape[0]
+    chunk = 128
+    count = query_count // chunk
+    cols, fcols = (width // recs, width // peers)
+    f32 = jnp.float32
+    small = pltpu.VMEM((count, taps, chunk), f32)
+    block = pltpu.VMEM((query_count, cols), f32)
+    scratch = [pltpu.VMEM((recs >> k, query_count, cols), f32) for k in range(bits)]
+    scratch += [pltpu.VMEM((recs >> (k + 1), query_count, cols), f32) for k in range(bits)]
+    scratch += [small] * (2 * bits) + [block] * 3 + [small] * 3
+    scratch += [
+        pltpu.VMEM((peers, row_count, fcols), f32),
+        pltpu.VMEM((peers - 1, row_count, fcols), f32),
+    ]
+    dma = pltpu.SemaphoreType.DMA
+    scratch += [dma((bits, 2, count))] * 2 + [dma((2, count))] * 4 + [dma((peers - 1,))] * 2
+    vmem = pl.BlockSpec(memory_space=pltpu.VMEM)
+    return pl.pallas_call(
+        functools.partial(gradient_kernel, (tms, peers, recs, chunk), scale),
+        out_shape=(
+            jax.ShapeDtypeStruct((row_count, fcols), jnp.bfloat16),
+            jax.ShapeDtypeStruct((query_count, cols), jnp.bfloat16),
+            jax.ShapeDtypeStruct((taps, query_count), f32),
+        ),
+        in_specs=[vmem] * 4,
+        out_specs=(vmem,) * 3,
+        scratch_shapes=scratch,
+        compiler_params=pltpu.CompilerParams(
+            collective_id=0, has_side_effects=True, vmem_limit_bytes=60 * 1024 * 1024
+        ),
+        name="gradients",
+    )(score_grad, frame_rows, queries, kernel_part)
 
 
 def tap_sum(kernel, padded, row_count, flipped):
@@ -107,22 +383,16 @@
     padded = wide[rim_width : rim_width + row_count + 2 * rim_width]
     score_grad = tap_sum(kernel, grad_pad, row_count, True)
     score_grad = jnp.where(is_valid[:, None], score_grad, 0.0).astype(jnp.bfloat16)
-    frame_part = jnp.dot(score_grad, queries, preferred_element_type=jnp.float32)
-    frame_sum = lax.psum_scatter(frame_part, "query", scatter_dimension=1, tiled=True)
-    grad_frames = (frame_sum * logit_scale).astype(jnp.bfloat16)[None]
-    query_part = lax.dot_general(
-        score_grad, frame_rows, (((0,), (0,)), ((), ())), preferred_element_type=jnp.float32
-    )
     kernel_part = jnp.stack(
         [
             jnp.sum(map_grad * padded[offset : offset + row_count], axis=0)
             for offset in range(tap_count)
         ]
     )
-    query_cols = lax.psum_scatter(query_part, "rec", scatter_dimension=1, tiled=True)
-    query_cols, grad_kernel = lax.psum((query_cols, lax.psum(kernel_part, "rec")), "tm")
-    grad_queries = (query_cols * logit_scale).astype(jnp.bfloat16)
-    return (grad_frames, grad_queries, grad_kernel)
+    grad_frames, grad_queries, grad_kernel = gradients(
+        score_grad, frame_rows, queries, kernel_part, logit_scale
+    )
+    return (grad_frames[None], grad_queries, grad_kernel)
 
 
 def solution(mesh):

time: 355 us -> 256 us (0.72)
  waiting for transfers between devices: 227 us -> 1.59 us
  Pallas kernels: 0 us -> 160 us
  between operations: 14.8 us -> 1.55 us
  matrix products: 22.9 us -> 10.2 us
  other arithmetic: 70.2 us -> 64.1 us
    pallas_call x0 -> x1, Pallas kernels: none -> 160 us  [gradients(): pl.pallas_call(functools.partial(gradient_kernel, (tms, peers, recs, chun...]
    psum x2 -> x0, waiting for transfers between devices: 118 us -> none  [the longest x1 97.2 us: per_device(): lax.psum((query_cols, lax.psum(kernel_part, 'rec')), 'tm')]
    reduce_scatter x2 -> x0, waiting for transfers between devices: 108 us -> none  [the longest x1 73.9 us: per_device(): lax.psum_scatter(query_part, 'rec', scatter_dimension=1, tiled=True)]
    dot_general x2 -> x0, matrix products: 12.7 us -> none  [the longest x1 6.85 us: per_device(): lax.dot_general(score_grad, frame_rows, (((0,), (0,)), ((), ())), preferr...]
    unnamed x37 -> x11, local copies, waits for them, and re-layouts: 1.8 us -> 5.87 us
    another operation x1, local copies, waits for them, and re-layouts: 7.47 us -> 3.54 us  [per_device(): jnp.stack([jnp.sum(map_grad * padded[offset:offset + row_count], axis=0)...]
  transfers between devices with their start and end apart: 7 -> 3, of which waited for: 5 -> 1; matrix products, arithmetic and copies ran while one was open for 6% -> 3% of each run, Pallas kernels for 0% -> 0%
where the time goes in v2:
time: 256 us
  Pallas kernels  160 us (62%)
  other arithmetic  64.1 us (25%)
  matrix products  10.2 us (4%)
  local copies, waits for them, and re-layouts  9.82 us (4%)
  starting transfers between devices  8.91 us (3%)
    pallas_call x1, Pallas kernels, gradients(): pl.pallas_call(functools.partial(gradient_kernel, (tms, peers, recs, chun...  160 us
    reduce_max x1, other arithmetic, row_softmax(): local_top = jnp.max(smooth, axis=1)  22.3 us
    convert_element_type x1, other arithmetic, per_device(): jnp.where(is_valid[:, None], score_grad, 0.0).astype(jnp.bfloat16)  18.7 us
    reduce_sum x3, other arithmetic, per_device(): jnp.sum(map_grad * padded[offset:offset + row_count], axis=0)  18.1 us
    dot_general x2, matrix products, scored(): lax.dot_general(rows, queries, (((1,), (1,)), ((), ())), preferred_elemen...  10.2 us
    unnamed x11, local copies, waits for them, and re-layouts  5.87 us
    ppermute x1, starting transfers between devices, halo_rows(): before = lax.ppermute(x[x.shape[0] - width:], axis, up)  5.59 us
  transfers between devices with their start and end apart: 3, of which 1 were waited for; matrix products, arithmetic and copies ran while one was open for 3% of the time, Pallas kernels for 0%

profile of v2, /device:TPU:0, one launch (start us, length us, event | category | flops | bytes accessed | tf_op | source)
XLA Modules:
  0.0 256.1 jit_solution(17256153033616508365)
XLA Ops:
  0.6 0.0 copy-start.1
  0.6 0.0 copy-start.2
  0.7 0.8 convert_element_type.30
  1.4 1.5 bitcast_convert_fusion
  2.9 0.1 broadcast_in_dim.54
  3.1 1.3 collective-permute-start.1
  4.4 5.6 %collective-permute-start = (f32[32,1152]{1,0:T(8,128)S(1)}, f32[32,1152]{1,0:T(8,128)S(1)}, u32[]{:S(2)}, u32[]{:S(2)}) collective-permute-start(f32[32,1152]{1,0:T(8,128)S(1)} %get-tuple-element.59), channel_id=1, source_target_pairs={{0,8},{8,16},{16,24},{1,9},{9,17},{17,25},{2,10},{10,18},{18,26},{... | collective-permute-start | bytes 442376 | tf_op jit(solution)/shard_map/ppermute | solution.py:26
  10.0 0.1 fusion.114
  10.1 0.1 fusion.113
  10.9 6.5 %convolution_multiply_fusion = f32[512,2048]{1,0:T(8,128)} fusion(bf16[2048,1024]{1,0:T(8,128)(2,1)} %qu_ref.1, bf16[1,512,1024]{2,1,0:T(8,128)(2,1)S(1)} %copy-done.1), kind=kOutput, calls=%fused_computation.200 | convolution fusion | flops 2148532224 | bytes 9437184 | tf_op jit(solution)/shard_map/dot_general | solution.py:356
  17.4 0.0 copy-start
  17.4 0.0 collective-permute-done.1
  17.4 0.0 collective-permute-done
  17.4 0.1 convert_reduce_fusion
  17.6 3.7 %convolution_multiply_fusion.1 = f32[64,2048]{1,0:T(8,128)S(1)} fusion(bf16[2048,1024]{1,0:T(8,128)(2,1)} %qu_ref.1, bf16[32,1024]{1,0:T(8,128)(2,1)S(1)} %slice.1206, bf16[32,1024]{1,0:T(8,128)(2,1)S(1)} %slice.1207), kind=kOutput, calls=%fused_computation.201 | convolution fusion | flops 268828672 | bytes 4849664 | tf_op jit(solution)/shard_map/dot_general | solution.py:356
  21.4 0.4 maximum_select_fusion
  21.8 22.3 %fusion.110 = (f32[544]{0:T(1024)S(1)}, f32[544,2048]{1,0:T(8,128)S(1)}) fusion(f32[576,2048]{1,0:T(8,128)S(1)} %maximum_select_fusion, f32[2048]{0:T(1024)S(1)} %bitcast.104, f32[2048]{0:T(1024)S(1)} %bitcast.106, f32[2048]{0:T(1024)S(1)} %bitcast.110, f32[2048]{0:T(1024)S(1)} %bitcast.112, f32[2048]{0:T(1024)S(1)} %bitcast.114, f32[2048]{0:T(1024)S(1)} %bitcast.116, ...), kind=kLoop, calls=%fused_computation.229 | loop fusion | flops 73530848 | bytes 151791744 | tf_op jit(solution)/shard_map/reduce_max | solution.py:322
  44.0 0.0 copy-start.3
  44.0 0.7 exponential_reduce_fusion
  44.8 2.0 collective-permute-start.2
  46.8 0.1 pad_add_fusion
  46.9 1.6 collective-permute-done.2
  48.5 1.5 subtract_select_fusion
  50.0 5.3 %fusion.49 = (f32[2048]{0:T(1024)S(1)}, f32[2048]{0:T(1024)S(1)}, f32[2048]{0:T(1024)S(1)}, f32[2048]{0:T(1024)S(1)}, f32[2048]{0:T(1024)S(1)}, /*index=5*/f32[2...) fusion(f32[576,2048]{1,0:T(8,128)S(1)} %maximum_select_fusion, f32[544,2048]{1,0:T(8,128)S(1)} %subtract_select_fusion), kind=kLoop, calls=%fused_computation.103 | loop fusion | flops 18855936 | bytes 42016768 | tf_op jit(solution)/shard_map/reduce_sum | solution.py:388
  55.3 5.0 %fusion.32 = (f32[2048]{0:T(1024)S(1)}, f32[2048]{0:T(1024)S(1)}, f32[2048]{0:T(1024)S(1)}, f32[2048]{0:T(1024)S(1)}, f32[2048]{0:T(1024)S(1)}, /*index=5*/f32[2...) fusion(f32[576,2048]{1,0:T(8,128)S(1)} %maximum_select_fusion, f32[544,2048]{1,0:T(8,128)S(1)} %subtract_select_fusion), kind=kLoop, calls=%fused_computation.69 | loop fusion | flops 18855936 | bytes 42016768 | tf_op jit(solution)/shard_map/reduce_sum | solution.py:388
  60.3 7.8 %fusion.40 = (f32[2048]{0:T(1024)S(1)}, f32[2048]{0:T(1024)S(1)}, f32[2048]{0:T(1024)S(1)}, f32[2048]{0:T(1024)S(1)}, f32[2048]{0:T(1024)S(1)}, /*index=5*/f32[2...) fusion(f32[576,2048]{1,0:T(8,128)S(1)} %maximum_select_fusion, ...), kind=kLoop, calls=%fused_computation.85 | loop fusion | flops 31426560 | bytes 67231744 | tf_op jit(solution)/shard_map/reduce_sum | solution.py:388
  68.1 18.7 %fusion.67.sg_ref = bf16[512,2048]{1,0:T(8,128)(2,1)} fusion(f32[544,2048]{1,0:T(8,128)S(1)} %subtract_select_fusion, f32[2048]{0:T(1024)S(1)} %bitcast.105, f32[2048]{0:T(1024)S(1)} %bitcast.107, f32[2048]{0:T(1024)S(1)} %bitcast.111, f32[2048]{0:T(1024)S(1)} %bitcast.113, f32[2048]{0:T(1024)S(1)} %bitcast.115, f32[2048]{0:T(1024)S(1)} %bitcast.117, ...), kind=kLoop, calls=%fused_computation.137 | loop fusion | flops 70254592 | bytes 140780032 | tf_op jit(solution)/shard_map/convert_element_type | solution.py:385
  86.8 3.5 %stack.147.kp_ref = f32[33,2048]{1,0:T(8,128)} concatenate(f32[1,2048]{1,0:T(1,128)S(1)} %bitcast.156, f32[1,2048]{1,0:T(1,128)S(1)} %bitcast.173, f32[1,2048]{1,0:T(1,128)S(1)} %bitcast.174, f32[1,2048]{1,0:T(1,128)S(1)} %bitcast.175, f32[1,2048]{1,0:T(1,128)S(1)} %bitcast.176, f32[1,2048]{1,0:T(1,128)S(1)} %bitcast.177, f32[1,2048]{1,0:T(1,128)S(1)} %bitcast.178, ...), dimensions={0} | concatenate | bytes 540672 | tf_op jit(solution)/shard_map/stack | solution.py:386
  90.3 159.9 %gradients.1 = (bf16[512,512]{1,0:T(8,128)(2,1)}, bf16[2048,256]{1,0:T(8,128)(2,1)}, f32[33,2048]{1,0:T(8,128)}) custom-call(bf16[512,2048]{1,0:T(8,128)(2,1)} %fusion.67.sg_ref, bf16[512,1024]{1,0:T(8,128)(2,1)} %bitcast.78, bf16[2048,1024]{1,0:T(8,128)(2,1)} %qu_ref.1, f32[33,2048]{1,0:T(8,128)} %stack.147.kp_ref), custom_call_target="tpu_custom_call" | custom-call | tf_op jit(solution)/shard_map/gradients/pallas_call | solution.py:287
  250.2 1.9 copy.12
  252.1 2.3 copy.13
  254.4 1.7 copy.14
  (17 shorter events, 0.2 us)
Async XLA Ops:
  0.6 10.2 %copy-start.1 = (bf16[1,512,1024]{2,1,0:T(8,128)(2,1)S(1)}, bf16[1,512,1024]{2,1,0:T(8,128)(2,1)}, u32[]{:S(2)}) copy-start(bf16[1,512,1024]{2,1,0:T(8,128)(2,1)} %param.5) | copy-start | bytes 3145732
  0.6 9.3 %copy-start.2 = (f32[33,2048]{1,0:T(8,128)S(1)}, f32[33,2048]{1,0:T(8,128)}, u32[]{:S(2)}) copy-start(f32[33,2048]{1,0:T(8,128)} %param.7) | copy-start | bytes 811012
  3.1 14.3 %collective-permute-start.1 = (f32[32,1152]{1,0:T(8,128)S(1)}, f32[32,1152]{1,0:T(8,128)S(1)}, u32[]{:S(2)}, u32[]{:S(2)}) collective-permute-start(f32[32,1152]{1,0:T(8,128)S(1)} %get-tuple-element.58), channel_id=1, source_target_pairs={{8,0},{16,8},{24,16},{9,1},{17,9},{25,17},{10,2},{18,10},{26,18},{... | collective-permute-start | bytes 442376 | tf_op jit(solution)/shard_map/ppermute | solution.py:27
  4.4 13.0 %collective-permute-start = (f32[32,1152]{1,0:T(8,128)S(1)}, f32[32,1152]{1,0:T(8,128)S(1)}, u32[]{:S(2)}, u32[]{:S(2)}) collective-permute-start(f32[32,1152]{1,0:T(8,128)S(1)} %get-tuple-element.59), channel_id=1, source_target_pairs={{0,8},{8,16},{16,24},{1,9},{9,17},{17,25},{2,10},{10,18},{18,26},{... | collective-permute-start | bytes 442376 | tf_op jit(solution)/shard_map/ppermute | solution.py:26
  17.4 4.0 %copy-start = (f32[512,2048]{1,0:T(8,128)S(1)}, f32[512,2048]{1,0:T(8,128)}, u32[]{:S(2)}) copy-start(f32[512,2048]{1,0:T(8,128)} %convolution_multiply_fusion) | copy-start | bytes 12582916
  44.0 2.8 %copy-start.3 = (s32[1,512]{1,0:T(1,128)S(1)}, s32[1,512]{1,0:T(1,128)}, u32[]{:S(2)}) copy-start(s32[1,512]{1,0:T(1,128)} %param.8) | copy-start | bytes 6148
  44.8 3.7 %collective-permute-start.2 = (f32[2,544]{1,0:T(2,128)S(1)}, f32[2,544]{1,0:T(2,128)S(1)}, u32[]{:S(2)}, u32[]{:S(2)}) collective-permute-start(f32[2,544]{1,0:T(2,128)S(1)} %pad_maximum_fusion.2), channel_id=1, source_target_pairs={{0,4},{4,0},{1,5},{5,1},{2,6},{6,2},{3,7},{7,3},{8,12},{12,8},{9,1... | collective-permute-start | bytes 13064 | tf_op jit(solution)/shard_map/ppermute | solution.py:17

commit v3 on v2

--- a/solution.py
+++ b/solution.py
@@ -28,6 +28,106 @@
     return lax.optimization_barrier((before, after))
 
 
+GROUPS = 4
+LANES = 128
+
+
+def spread_taps(kern_ref, lanes):
+    taps = kern_ref.shape[0]
+    return [jnp.broadcast_to(kern_ref[j : j + 1, lanes], (8, LANES)) for j in range(taps)]
+
+
+def tap_block(load, taps, flipped):
+    count = len(taps)
+    sums = [None] * GROUPS
+    for o in range(8 * (GROUPS - 1) + count):
+        v = load(o)
+        for i in range(GROUPS):
+            j = o - 8 * i
+            if 0 <= j < count:
+                term = taps[count - 1 - j if flipped else j] * v
+                sums[i] = term if sums[i] is None else sums[i] + term
+    return sums
+
+
+def smooth_kernel(scale, x_ref, q_ref, kern_ref, valid_ref, sc_ref, e_ref, top_ref, total_ref):
+    tiles, ext, _ = e_ref.shape
+    wide = x_ref.shape[0]
+    pair = 2 * LANES
+    block = 8 * GROUPS
+
+    top_ref[...] = jnp.full_like(top_ref, -jnp.inf)
+
+    def score(c, carry):
+        rows = pl.ds(pl.multiple_of(c * pair, pair), pair)
+        part = lax.dot_general(
+            x_ref[...],
+            q_ref[rows, :],
+            (((1,), (1,)), ((), ())),
+            preferred_element_type=jnp.float32,
+        )
+        for h in range(2):
+            one = part[:, h * LANES : (h + 1) * LANES] * scale
+            sc_ref[2 * c + h] = jnp.where(valid_ref[...] > 0, one, 0.0)
+        return carry
+
+    lax.fori_loop(0, tiles // 2, score, 0)
+
+    def smoothed(c, carry):
+        taps = spread_taps(kern_ref, pl.ds(pl.multiple_of(c * LANES, LANES), LANES))
+
+        def body(g, carry):
+            base = pl.multiple_of(g * block, block)
+            sums = tap_block(lambda o: sc_ref[c, pl.ds(base + o, 8), :], taps, False)
+            for i in range(GROUPS):
+                rows = pl.ds(base + 8 * i, 8)
+                e_ref[c, rows, :] = sums[i]
+                top_ref[rows, :] = jnp.maximum(top_ref[rows, :], sums[i])
+            return carry
+
+        return lax.fori_loop(0, ext // block, body, carry)
+
+    lax.fori_loop(0, tiles, smoothed, 0)
+
+    def finish(g, carry):
+        rows = pl.ds(pl.multiple_of(g * block, block), block)
+        top = jnp.max(top_ref[rows, :], axis=1, keepdims=True)
+        top = jnp.broadcast_to(top, (block, LANES))
+        top_ref[rows, :] = top
+        total = jnp.zeros((block, LANES), jnp.float32)
+        for c in range(tiles):
+            e = jnp.exp(e_ref[c, rows, :] - top)
+            e_ref[c, rows, :] = e
+            total = total + e
+        total = jnp.sum(total, axis=1, keepdims=True)
+        total_ref[rows, :] = jnp.broadcast_to(total, (block, LANES))
+        return carry
+
+    lax.fori_loop(0, ext // block, finish, 0)
+
+
+def smooth_exp(rows, queries, kernel, valid, scale):
+    wide = rows.shape[0]
+    query_count = queries.shape[0]
+    ext = wide - (kernel.shape[0] // 2) * 2
+    tiles = query_count // LANES
+    f32 = jnp.float32
+    vmem = pl.BlockSpec(memory_space=pltpu.VMEM)
+    return pl.pallas_call(
+        functools.partial(smooth_kernel, scale),
+        out_shape=(
+            jax.ShapeDtypeStruct((tiles, wide, LANES), f32),
+            jax.ShapeDtypeStruct((tiles, ext, LANES), f32),
+            jax.ShapeDtypeStruct((ext, LANES), f32),
+            jax.ShapeDtypeStruct((ext, LANES), f32),
+        ),
+        in_specs=[vmem] * 4,
+        out_specs=(vmem,) * 4,
+        compiler_params=pltpu.CompilerParams(vmem_limit_bytes=40 * 1024 * 1024),
+        name="smooth",
+    )(rows, queries, kernel, valid)
+
+
 MESH = pl.DeviceIdType.MESH
 
 
@@ -36,7 +136,8 @@
 
 
 def gradient_kernel(
-    dims, scale, sg_ref, fr_ref, qu_ref, kp_ref, gf_ref, gq_ref, gk_ref, *scratch
+    dims, scale, sc_ref, e_ref, f_ref, lab_ref, fr_ref, qu_ref, kern_ref, gf_ref, gq_ref, gk_ref,
+    *scratch,
 ):
     tms, peers, recs, chunk = dims
     bits = recs.bit_length() - 1
@@ -44,8 +145,8 @@
     arrived, scratch = scratch[:bits], scratch[bits:]
     kacc, scratch = scratch[:bits], scratch[bits:]
     karrived, scratch = scratch[:bits], scratch[bits:]
-    (mid, outer, inner, kmid, kouter, kinner, fpart, fin) = scratch[:8]
-    (rec_send, rec_recv, in_send, out_recv, out_send, inn_recv, f_send, f_recv) = scratch[8:]
+    (mid, outer, inner, kmid, kouter, kinner, fpart, fin, sg_ref, grad, ksum) = scratch[:11]
+    (rec_send, rec_recv, in_send, out_recv, out_send, inn_recv, f_send, f_recv) = scratch[11:]
 
     t = lax.axis_index("tm")
     y = lax.axis_index("query")
@@ -157,7 +258,61 @@
             copy(kinner.at[c], kinner.at[c], out_send.at[1, c], inn_recv.at[1, c], device),
         )
 
+    taps_n = kern_ref.shape[0]
+    rim = taps_n // 2
+    block = 8 * GROUPS
+    ext = grad.shape[0]
+    lane = lax.broadcasted_iota(jnp.int32, (8, LANES), 1) + y * queries
+
+    def map_gradient(c):
+        first = lane + c * chunk
+
+        def body(g, carry):
+            for i in range(GROUPS):
+                rows = pl.ds(pl.multiple_of(g * block + 8 * i, 8), 8)
+                hit = jnp.where(lab_ref[rows, :] == first, 1.0, 0.0)
+                factor = f_ref[rows, :]
+                value = e_ref[c, rows, :] * jnp.maximum(factor, 0.0) - hit
+                grad[rows, :] = jnp.where(factor >= 0.0, value, 0.0)
+            return carry
+
+        lax.fori_loop(0, ext // block, body, 0)
+
+    def score_gradient(c):
+        taps = spread_taps(kern_ref, at(c))
+
+        def body(g, carry):
+            base = pl.multiple_of(g * block, block)
+            sums = tap_block(lambda o: grad[pl.ds(base + o, 8), :], taps, True)
+            valid = f_ref[pl.ds(base + rim, block), :] >= 0.0
+            total = jnp.where(valid, jnp.concatenate(sums, axis=0), 0.0)
+            sg_ref[pl.ds(base, block), at(c)] = total.astype(jnp.bfloat16)
+            return carry
+
+        lax.fori_loop(0, row_count // block, body, 0)
+
+    def tap_gradient(c):
+        def body(g, sums):
+            base = pl.multiple_of(g * block, block)
+            held = [grad[pl.ds(base + rim + 8 * i, 8), :] for i in range(GROUPS)]
+            sums = list(sums)
+            for o in range(8 * (GROUPS - 1) + taps_n):
+                v = sc_ref[c, pl.ds(base + rim + o, 8), :]
+                for i in range(GROUPS):
+                    j = o - 8 * i
+                    if 0 <= j < taps_n:
+                        sums[j] = sums[j] + held[i] * v
+            return tuple(sums)
+
+        zero = jnp.zeros((8, LANES), jnp.float32)
+        sums = lax.fori_loop(0, row_count // block, body, (zero,) * taps_n)
+        for j in range(taps_n):
+            ksum[j : j + 1, :] = jnp.sum(sums[j], axis=0, keepdims=True)
+
     def start(c):
+        map_gradient(c)
+        score_gradient(c)
+        tap_gradient(c)
         part = lax.dot_general(
             sg_ref[:, at(c)],
             fr_ref[...],
@@ -167,7 +322,7 @@
         for p in range(recs):
             j = bit_reversed(p, bits)
             acc[0][p, at(c), :] = part[:, j * cols : (j + 1) * cols]
-        kacc[0][c] = kp_ref[:, at(c)]
+        kacc[0][c] = ksum[...]
         for one in rec_copies(0, c):
             one.start()
 
@@ -217,23 +372,31 @@
         gq_ref[at(c), :] = (inner[at(c), :] * scale).astype(gq_ref.dtype)
         gk_ref[:, at(c)] = kinner[c]
 
-    for d in range(1, peers):
-        f_compute(lax.rem(y + d, peers))
-        f_copy(d).start()
-
-    lag = bits + 4
-    stages = [(0, start)]
-    stages += [(k, functools.partial(exchange, k)) for k in range(1, bits)]
-    stages += [(bits, gather_in), (lag, spread_out)]
+    def send_frames():
+        for d in range(1, peers):
+            f_compute(lax.rem(y + d, peers))
+            f_copy(d).start()
+
+    reach = half - 1
+    away = jnp.where(low, reach - t, t - half)
+    in_lag = bits + 1 + 2 * (reach - away)
+    out_lag = bits + 3 + 2 * (reach + away)
+    last_lag = bits + 3 + 4 * reach
+    stages = [(0, start), (out_lag, spread_out), (in_lag, gather_in)]
+    stages += [(k, functools.partial(exchange, k)) for k in range(bits - 1, 0, -1)]
 
     def step(s, carry):
+        @pl.when(s == count)
+        def _():
+            send_frames()
+
         for delay, stage in stages:
             @pl.when((s >= delay) & (s < count + delay))
             def _(stage=stage, delay=delay):
                 stage(s - delay)
         return carry
 
-    lax.fori_loop(0, count + lag, step, 0)
+    lax.fori_loop(0, count + last_lag, step, 0)
 
     f_compute(y)
     for d in range(1, peers):
@@ -262,13 +425,13 @@
     lax.fori_loop(0, count, drain, 0)
 
 
-def gradients(score_grad, frame_rows, queries, kernel_part, scale):
+def gradients(scores, exps, factor, labels, frame_rows, queries, kernel, scale):
     tms, peers, recs = (lax.axis_size("tm"), lax.axis_size("query"), lax.axis_size("rec"))
     bits = recs.bit_length() - 1
     row_count, width = frame_rows.shape
     query_count = queries.shape[0]
-    taps = kernel_part.shape[0]
-    chunk = 128
+    taps = kernel.shape[0]
+    chunk = LANES
     count = query_count // chunk
     cols, fcols = (width // recs, width // peers)
     f32 = jnp.float32
@@ -280,6 +443,9 @@
     scratch += [
         pltpu.VMEM((peers, row_count, fcols), f32),
         pltpu.VMEM((peers - 1, row_count, fcols), f32),
+        pltpu.VMEM((row_count, query_count), jnp.bfloat16),
+        pltpu.VMEM((exps.shape[1], chunk), f32),
+        pltpu.VMEM((taps, chunk), f32),
     ]
     dma = pltpu.SemaphoreType.DMA
     scratch += [dma((bits, 2, count))] * 2 + [dma((2, count))] * 4 + [dma((peers - 1,))] * 2
@@ -291,23 +457,14 @@
             jax.ShapeDtypeStruct((query_count, cols), jnp.bfloat16),
             jax.ShapeDtypeStruct((taps, query_count), f32),
         ),
-        in_specs=[vmem] * 4,
+        in_specs=[vmem] * 7,
         out_specs=(vmem,) * 3,
         scratch_shapes=scratch,
         compiler_params=pltpu.CompilerParams(
             collective_id=0, has_side_effects=True, vmem_limit_bytes=60 * 1024 * 1024
         ),
         name="gradients",
-    )(score_grad, frame_rows, queries, kernel_part)
-
-
-def tap_sum(kernel, padded, row_count, flipped):
-    tap_count = kernel.shape[0]
-    running = jnp.zeros((row_count, padded.shape[1]), jnp.float32)
-    for offset in range(tap_count):
-        begin_row = tap_count - 1 - offset if flipped else offset
-        running = running + kernel[offset][None, :] * padded[begin_row : begin_row + row_count]
-    return running
+    )(scores, exps, factor, labels, frame_rows, queries, kernel)
 
 
 def combine_stats(first_pair, second_pair):
@@ -316,14 +473,6 @@
         second_pair[0] - top_value
     )
     return jnp.stack([top_value, total_value])
-
-
-def row_softmax(smooth):
-    local_top = jnp.max(smooth, axis=1)
-    local_total = jnp.sum(jnp.exp(smooth - local_top[:, None]), axis=1)
-    stats = merged(jnp.stack([local_top, local_total]), "query", combine_stats)
-    top_value, total_value = stats[0], stats[1]
-    return jnp.exp(smooth - top_value[:, None]) / total_value[:, None]
 
 
 def per_device(frames, queries, kernel, labels, lengths):
@@ -337,9 +486,6 @@
     rim_width = tap_count // 2
     logit_scale = 10.0 / math.sqrt(width)
     frame_start = lax.axis_index("tm") * row_count
-    is_valid = frame_start + jnp.arange(row_count, dtype=jnp.int32) < length_now
-    query_start = lax.axis_index("query") * query_count
-    query_ids = query_start + jnp.arange(query_count, dtype=jnp.int32)
     halo = 2 * rim_width
     tagged = jnp.concatenate(
         [
@@ -351,20 +497,10 @@
     before, after = halo_rows(tagged, "tm", halo)
     rim_rows = jnp.concatenate([before[:, :width], after[:, :width]]).astype(jnp.bfloat16)
 
-    def scored(rows):
-        return (
-            lax.dot_general(
-                rows, queries, (((1,), (1,)), ((), ())), preferred_element_type=jnp.float32
-            )
-            * logit_scale
-        )
-
-    inner = scored(frame_rows)
-    rim = scored(rim_rows)
-    wide = jnp.concatenate([rim[:halo], inner, rim[halo:]])
+    wide_rows = jnp.concatenate([rim_rows[:halo], frame_rows, rim_rows[halo:]])
     wide_frames = frame_start - halo + jnp.arange(row_count + 2 * halo, dtype=jnp.int32)
     wide_valid = (wide_frames >= 0) & (wide_frames < length_now)
-    wide = jnp.where(wide_valid[:, None], wide, 0.0)
+    wide_valid = jnp.broadcast_to(wide_valid[:, None], (wide_valid.shape[0], LANES))
     label_pad = jnp.concatenate(
         [
             before[halo - rim_width :, width].astype(jnp.int32),
@@ -375,22 +511,17 @@
     ext_rows = row_count + 2 * rim_width
     ext_frames = frame_start - rim_width + jnp.arange(ext_rows, dtype=jnp.int32)
     ext_valid = (ext_frames >= 0) & (ext_frames < length_now)
-    smooth = tap_sum(kernel, wide, ext_rows, False)
-    softmax_out = row_softmax(smooth)
-    positive = (label_pad[:, None] == query_ids[None, :]).astype(jnp.float32)
-    grad_pad = jnp.where(ext_valid[:, None], softmax_out - positive, 0.0)
-    map_grad = grad_pad[rim_width : rim_width + row_count]
-    padded = wide[rim_width : rim_width + row_count + 2 * rim_width]
-    score_grad = tap_sum(kernel, grad_pad, row_count, True)
-    score_grad = jnp.where(is_valid[:, None], score_grad, 0.0).astype(jnp.bfloat16)
-    kernel_part = jnp.stack(
-        [
-            jnp.sum(map_grad * padded[offset : offset + row_count], axis=0)
-            for offset in range(tap_count)
-        ]
+    scores, exps, local_top, local_total = smooth_exp(
+        wide_rows, queries, kernel, wide_valid.astype(jnp.float32), logit_scale
     )
+    top = local_top[:, 0]
+    stats = merged(jnp.stack([top, local_total[:, 0]]), "query", combine_stats)
+    factor = jnp.exp(top - stats[0]) / stats[1]
+    factor = jnp.where(ext_valid, factor, -1.0)
+    factor = jnp.broadcast_to(factor[:, None], (ext_rows, LANES))
+    label_wide = jnp.broadcast_to(label_pad[:, None], (ext_rows, LANES))
     grad_frames, grad_queries, grad_kernel = gradients(
-        score_grad, frame_rows, queries, kernel_part, logit_scale
+        scores, exps, factor, label_wide, frame_rows, queries, kernel, logit_scale
     )
     return (grad_frames[None], grad_queries, grad_kernel)
 

time: 256 us -> 140 us (0.55)
  other arithmetic: 64.1 us -> 2.73 us
  Pallas kernels: 160 us -> 110 us
  matrix products: 10.2 us -> 0 us
  waiting for transfers between devices: 1.59 us -> 4.28 us
    pallas_call x1, Pallas kernels: 160 us -> 88 us  [gradients(): pl.pallas_call(functools.partial(gradient_kernel, (tms, peers, recs, chun...]
    pallas_call x0 -> x1, Pallas kernels: none -> 22.5 us  [smooth_exp(): pl.pallas_call(functools.partial(smooth_kernel, scale), out_shape=(jax.Sh...]
    reduce_max x1 -> x0, other arithmetic: 22.3 us -> none  [row_softmax(): local_top = jnp.max(smooth, axis=1)]
    reduce_sum x4 -> x0, other arithmetic: 18.8 us -> none  [the longest x3 18.1 us: per_device(): jnp.sum(map_grad * padded[offset:offset + row_count], axis=0)]
    convert_element_type x1, other arithmetic: 18.7 us -> 0.01 us  [per_device(): wide_valid.astype(jnp.float32)]
    dot_general x2 -> x0, matrix products: 10.2 us -> none  [scored(): lax.dot_general(rows, queries, (((1,), (1,)), ((), ())), preferred_elemen...]
    another operation x3 -> x2, local copies, waits for them, and re-layouts: 3.55 us -> 0.01 us  [per_device(): stats = merged(jnp.stack([top, local_total[:, 0]]), 'query', combine_stats)]
    unnamed x11 -> x15, local copies, waits for them, and re-layouts: 5.87 us -> 9.21 us
  transfers between devices with their start and end apart: 3 -> 3, of which waited for: 1 -> 3; matrix products, arithmetic and copies ran while one was open for 3% -> 0% of each run, Pallas kernels for 0% -> 0%
where the time goes in v3:
time: 140 us; the launch traced here: 139 us
  Pallas kernels  110 us (79%)
  local copies, waits for them, and re-layouts  11.7 us (8%)
  starting transfers between devices  8.75 us (6%)
  waiting for transfers between devices  4.28 us (3%)
  other arithmetic  2.73 us (2%)
  between operations  1.47 us (1%)
    pallas_call x1, Pallas kernels, gradients(): pl.pallas_call(functools.partial(gradient_kernel, (tms, peers, recs, chun...  88 us
    pallas_call x1, Pallas kernels, smooth_exp(): pl.pallas_call(functools.partial(smooth_kernel, scale), out_shape=(jax.Sh...  22.5 us
    unnamed x15, local copies, waits for them, and re-layouts  9.21 us
    ppermute x1, starting transfers between devices, halo_rows(): before = lax.ppermute(x[x.shape[0] - width:], axis, up)  5.59 us
  transfers between devices with their start and end apart: 3, of which 3 were waited for; matrix products, arithmetic and copies ran while one was open for 0% of the time, Pallas kernels for 0%

profile of v3, /device:TPU:0, one launch (start us, length us, event | category | flops | bytes accessed | tf_op | source)
XLA Modules:
  0.0 139.4 jit_solution(2355271761249916299)
XLA Ops:
  0.6 0.7 convert_element_type.27
  1.3 1.5 %bitcast_convert_fusion = f32[512,1024]{1,0:T(8,128)S(1)} fusion(bf16[1,512,1024]{2,1,0:T(8,128)(2,1)} %param.5), kind=kLoop, calls=%fused_computation.31 | loop fusion | flops 524288 | bytes 3145728 | tf_op jit(solution)/shard_map/convert_element_type | solution.py:492
  2.8 0.0 copy-start.3
  2.8 0.1 broadcast_in_dim.16
  2.9 0.0 copy-start.2
  3.0 1.4 %collective-permute-start.1 = (f32[32,1152]{1,0:T(8,128)S(1)}, f32[32,1152]{1,0:T(8,128)S(1)}, u32[]{:S(2)}, u32[]{:S(2)}) collective-permute-start(f32[32,1152]{1,0:T(8,128)S(1)} %get-tuple-element.21), channel_id=1, source_target_pairs={{8,0},{16,8},{24,16},{9,1},{17,9},{25,17},{10,2},{18,10},{26,18},{... | collective-permute-start | bytes 442376 | tf_op jit(solution)/shard_map/ppermute | solution.py:27
  4.4 5.6 %collective-permute-start = (f32[32,1152]{1,0:T(8,128)S(1)}, f32[32,1152]{1,0:T(8,128)S(1)}, u32[]{:S(2)}, u32[]{:S(2)}) collective-permute-start(f32[32,1152]{1,0:T(8,128)S(1)} %get-tuple-element.22), channel_id=1, source_target_pairs={{0,8},{8,16},{16,24},{1,9},{9,17},{17,25},{2,10},{10,18},{18,26},{... | collective-permute-start | bytes 442376 | tf_op jit(solution)/shard_map/ppermute | solution.py:26
  10.7 1.2 collective-permute-done.1
  11.9 1.2 collective-permute-done
  13.1 0.1 convert_reduce_fusion
  13.2 0.0 copy-done.3
  13.2 0.1 pad_maximum_fusion.x_ref
  13.3 0.1 broadcast_in_dim.17.valid_ref
  13.5 0.0 copy-done.2
  13.5 0.0 copy-start
  13.5 2.2 %copy-done = bf16[2048,1024]{1,0:T(8,128)(2,1)S(1)} copy-done((bf16[2048,1024]{1,0:T(8,128)(2,1)S(1)}, bf16[2048,1024]{1,0:T(8,128)(2,1)}, u32[]{:S(2)}) %copy-start) | copy-done | bytes 4194328
  15.7 22.5 %smooth.1 = (f32[16,576,128]{2,1,0:T(8,128)}, f32[16,544,128]{2,1,0:T(8,128)S(1)}, f32[544,128]{1,0:T(8,128)S(1)}, f32[544,128]{1,0:T(8,128)S(1)}) custom-call(bf16[576,1024]{1,0:T(8,128)(2,1)S(1)} %pad_maximum_fusion.x_ref, bf16[2048,1024]{1,0:T(8,128)(2,1)S(1)} %copy-done, f32[33,2048]{1,0:T(8,128)S(1)} %copy-done.2, f32[576,128]{1,0:T(8,128)S(1)} %broadcast_in_dim.17.valid_ref), custom_call_target="tpu_custom_call" | custom-call | tf_op jit(solution)/shard_map/smooth/pallas_call | solution.py:116
  38.1 2.1 %copy-done.1 = f32[16,544,128]{2,1,0:T(8,128)} copy-done((f32[16,544,128]{2,1,0:T(8,128)}, f32[16,544,128]{2,1,0:T(8,128)S(1)}, u32[]{:S(2)}) %copy-start.1) | copy-done | bytes 4456472
  40.2 0.2 slice_reduce_fusion
  40.5 1.7 %collective-permute-start.2 = (f32[2,544]{1,0:T(2,128)S(1)}, f32[2,544]{1,0:T(2,128)S(1)}, u32[]{:S(2)}, u32[]{:S(2)}) collective-permute-start(f32[2,544]{1,0:T(2,128)S(1)} %pad_maximum_fusion.3), channel_id=1, source_target_pairs={{0,4},{4,0},{1,5},{5,1},{2,6},{6,2},{3,7},{7,3},{8,12},{12,8},{9,1... | collective-permute-start | bytes 13064 | tf_op jit(solution)/shard_map/ppermute | solution.py:17
  42.2 0.0 copy-done.5
  42.2 0.1 pad_add_fusion
  42.3 1.9 %collective-permute-done.2 = f32[2,544]{1,0:T(2,128)S(1)} collective-permute-done((f32[2,544]{1,0:T(2,128)S(1)}, f32[2,544]{1,0:T(2,128)S(1)}, u32[]{:S(2)}, u32[]{:S(2)}) %collective-permute-start.2) | collective-permute-done | bytes 4384 | tf_op jit(solution)/shard_map/ppermute | solution.py:17
  44.2 0.1 copy.11
  44.4 0.1 copy.13
  44.5 0.3 fusion.8
  44.8 0.9 broadcast_in_dim.38.lab_ref
  45.6 0.8 broadcast_in_dim.37.f_ref
  46.5 88.0 %gradients.1 = (bf16[512,512]{1,0:T(8,128)(2,1)}, bf16[2048,256]{1,0:T(8,128)(2,1)}, f32[33,2048]{1,0:T(8,128)}) custom-call(f32[16,576,128]{2,1,0:T(8,128)} %get-tuple-element.14.sc_ref, f32[16,544,128]{2,1,0:T(8,128)} %copy-done.1, f32[544,128]{1,0:T(8,128)} %broadcast_in_dim.37.f_ref, s32[544,128]{1,0:T(8,128)} %broadcast_in_dim.38.lab_ref, ...), custom_call_target="tpu_custom_call" | custom-call | tf_op jit(solution)/shard_map/gradients/pallas_call | solution.py:453
  134.5 1.9 %copy.18 = bf16[1,512,512]{2,1,0:T(8,128)(2,1)} copy(bf16[1,512,512]{2,1,0:T(8,128)(2,1)} %bitcast.13) | data formatting | bytes 1048576
  136.4 2.3 %copy.19 = bf16[2048,256]{1,0:T(8,128)(2,1)} copy(bf16[2048,256]{1,0:T(8,128)(2,1)} %get-tuple-element.33) | data formatting | bytes 2097152
  138.7 0.7 copy.20
  (12 shorter events, 0.1 us)
Async XLA Ops:
  2.8 10.4 %copy-start.3 = (bf16[1,512,1024]{2,1,0:T(8,128)(2,1)S(1)}, bf16[1,512,1024]{2,1,0:T(8,128)(2,1)}, u32[]{:S(2)}) copy-start(bf16[1,512,1024]{2,1,0:T(8,128)(2,1)} %param.5) | copy-start | bytes 3145732
  2.9 10.5 %copy-start.2 = (f32[33,2048]{1,0:T(8,128)S(1)}, f32[33,2048]{1,0:T(8,128)}, u32[]{:S(2)}) copy-start(f32[33,2048]{1,0:T(8,128)} %kern_ref.3) | copy-start | bytes 811012
  3.0 8.9 %collective-permute-start.1 = (f32[32,1152]{1,0:T(8,128)S(1)}, f32[32,1152]{1,0:T(8,128)S(1)}, u32[]{:S(2)}, u32[]{:S(2)}) collective-permute-start(f32[32,1152]{1,0:T(8,128)S(1)} %get-tuple-element.21), channel_id=1, source_target_pairs={{8,0},{16,8},{24,16},{9,1},{17,9},{25,17},{10,2},{18,10},{26,18},{... | collective-permute-start | bytes 442376 | tf_op jit(solution)/shard_map/ppermute | solution.py:27
  4.4 8.7 %collective-permute-start = (f32[32,1152]{1,0:T(8,128)S(1)}, f32[32,1152]{1,0:T(8,128)S(1)}, u32[]{:S(2)}, u32[]{:S(2)}) collective-permute-start(f32[32,1152]{1,0:T(8,128)S(1)} %get-tuple-element.22), channel_id=1, source_target_pairs={{0,8},{8,16},{16,24},{1,9},{9,17},{17,25},{2,10},{10,18},{18,26},{... | collective-permute-start | bytes 442376 | tf_op jit(solution)/shard_map/ppermute | solution.py:26
  13.5 2.2 %copy-start = (bf16[2048,1024]{1,0:T(8,128)(2,1)S(1)}, bf16[2048,1024]{1,0:T(8,128)(2,1)}, u32[]{:S(2)}) copy-start(bf16[2048,1024]{1,0:T(8,128)(2,1)} %qu_ref.1) | copy-start | bytes 12582916
  15.7 26.6 %copy-start.5 = (s32[1,512]{1,0:T(1,128)S(1)}, s32[1,512]{1,0:T(1,128)}, u32[]{:S(2)}) copy-start(s32[1,512]{1,0:T(1,128)} %param.8) | copy-start | bytes 6148
  38.1 2.1 %copy-start.1 = (f32[16,544,128]{2,1,0:T(8,128)}, f32[16,544,128]{2,1,0:T(8,128)S(1)}, u32[]{:S(2)}) copy-start(f32[16,544,128]{2,1,0:T(8,128)S(1)} %get-tuple-element.15.e_ref) | copy-start | bytes 13369348
  40.5 3.7 %collective-permute-start.2 = (f32[2,544]{1,0:T(2,128)S(1)}, f32[2,544]{1,0:T(2,128)S(1)}, u32[]{:S(2)}, u32[]{:S(2)}) collective-permute-start(f32[2,544]{1,0:T(2,128)S(1)} %pad_maximum_fusion.3), channel_id=1, source_target_pairs={{0,4},{4,0},{1,5},{5,1},{2,6},{6,2},{3,7},{7,3},{8,12},{12,8},{9,1... | collective-permute-start | bytes 13064 | tf_op jit(solution)/shard_map/ppermute | solution.py:17
  134.5 4.2 %copy-start.4 = (f32[33,2048]{1,0:T(8,128)S(1)}, f32[33,2048]{1,0:T(8,128)}, u32[]{:S(2)}) copy-start(f32[33,2048]{1,0:T(8,128)} %get-tuple-element.34) | copy-start | bytes 811012

commit v4 on v3

--- a/solution.py
+++ b/solution.py
@@ -7,25 +7,6 @@
 from jax.experimental import pallas as pl
 from jax.experimental.pallas import tpu as pltpu
 from jax.sharding import PartitionSpec as P
-
-
-def merged(x, axis, combine):
-    peers = lax.axis_size(axis)
-    step = 1
-    while step < peers:
-        swap = [(i, i ^ step) for i in range(peers)]
-        x = combine(x, lax.ppermute(x, axis, swap))
-        step *= 2
-    return x
-
-
-def halo_rows(x, axis, width):
-    peers = lax.axis_size(axis)
-    up = [(i, i + 1) for i in range(peers - 1)]
-    down = [(i + 1, i) for i in range(peers - 1)]
-    before = lax.ppermute(x[x.shape[0] - width :], axis, up)
-    after = lax.ppermute(x[:width], axis, down)
-    return lax.optimization_barrier((before, after))
 
 
 GROUPS = 4
@@ -50,84 +31,6 @@
     return sums
 
 
-def smooth_kernel(scale, x_ref, q_ref, kern_ref, valid_ref, sc_ref, e_ref, top_ref, total_ref):
-    tiles, ext, _ = e_ref.shape
-    wide = x_ref.shape[0]
-    pair = 2 * LANES
-    block = 8 * GROUPS
-
-    top_ref[...] = jnp.full_like(top_ref, -jnp.inf)
-
-    def score(c, carry):
-        rows = pl.ds(pl.multiple_of(c * pair, pair), pair)
-        part = lax.dot_general(
-            x_ref[...],
-            q_ref[rows, :],
-            (((1,), (1,)), ((), ())),
-            preferred_element_type=jnp.float32,
-        )
-        for h in range(2):
-            one = part[:, h * LANES : (h + 1) * LANES] * scale
-            sc_ref[2 * c + h] = jnp.where(valid_ref[...] > 0, one, 0.0)
-        return carry
-
-    lax.fori_loop(0, tiles // 2, score, 0)
-
-    def smoothed(c, carry):
-        taps = spread_taps(kern_ref, pl.ds(pl.multiple_of(c * LANES, LANES), LANES))
-
-        def body(g, carry):
-            base = pl.multiple_of(g * block, block)
-            sums = tap_block(lambda o: sc_ref[c, pl.ds(base + o, 8), :], taps, False)
-            for i in range(GROUPS):
-                rows = pl.ds(base + 8 * i, 8)
-                e_ref[c, rows, :] = sums[i]
-                top_ref[rows, :] = jnp.maximum(top_ref[rows, :], sums[i])
-            return carry
-
-        return lax.fori_loop(0, ext // block, body, carry)
-
-    lax.fori_loop(0, tiles, smoothed, 0)
-
-    def finish(g, carry):
-        rows = pl.ds(pl.multiple_of(g * block, block), block)
-        top = jnp.max(top_ref[rows, :], axis=1, keepdims=True)
-        top = jnp.broadcast_to(top, (block, LANES))
-        top_ref[rows, :] = top
-        total = jnp.zeros((block, LANES), jnp.float32)
-        for c in range(tiles):
-            e = jnp.exp(e_ref[c, rows, :] - top)
-            e_ref[c, rows, :] = e
-            total = total + e
-        total = jnp.sum(total, axis=1, keepdims=True)
-        total_ref[rows, :] = jnp.broadcast_to(total, (block, LANES))
-        return carry
-
-    lax.fori_loop(0, ext // block, finish, 0)
-
-
-def smooth_exp(rows, queries, kernel, valid, scale):
-    wide = rows.shape[0]
-    query_count = queries.shape[0]
-    ext = wide - (kernel.shape[0] // 2) * 2
-    tiles = query_count // LANES
-    f32 = jnp.float32
-    vmem = pl.BlockSpec(memory_space=pltpu.VMEM)
-    return pl.pallas_call(
-        functools.partial(smooth_kernel, scale),
-        out_shape=(
-            jax.ShapeDtypeStruct((tiles, wide, LANES), f32),
-            jax.ShapeDtypeStruct((tiles, ext, LANES), f32),
-            jax.ShapeDtypeStruct((ext, LANES), f32),
-            jax.ShapeDtypeStruct((ext, LANES), f32),
-        ),
-        in_specs=[vmem] * 4,
-        out_specs=(vmem,) * 4,
-        compiler_params=pltpu.CompilerParams(vmem_limit_bytes=40 * 1024 * 1024),
-        name="smooth",
-    )(rows, queries, kernel, valid)
-
-
 MESH = pl.DeviceIdType.MESH
 
 
@@ -136,7 +39,17 @@
 
 
 def gradient_kernel(
-    dims, scale, sc_ref, e_ref, f_ref, lab_ref, fr_ref, qu_ref, kern_ref, gf_ref, gq_ref, gk_ref,
+    dims,
+    scale,
+    halo_ref,
+    own_lab_ref,
+    len_ref,
+    fr_ref,
+    qu_ref,
+    kern_ref,
+    gf_ref,
+    gq_ref,
+    gk_ref,
     *scratch,
 ):
     tms, peers, recs, chunk = dims
@@ -146,7 +59,10 @@
     kacc, scratch = scratch[:bits], scratch[bits:]
     karrived, scratch = scratch[:bits], scratch[bits:]
     (mid, outer, inner, kmid, kouter, kinner, fpart, fin, sg_ref, grad, ksum) = scratch[:11]
-    (rec_send, rec_recv, in_send, out_recv, out_send, inn_recv, f_send, f_recv) = scratch[11:]
+    (sc_ref, e_ref, f_ref, lab_ref, valid_ref, x_ref, hin, stat, stat_in) = scratch[11:20]
+    scratch = scratch[20:]
+    (rec_send, rec_recv, in_send, out_recv, out_send, inn_recv, f_send, f_recv) = scratch[:8]
+    (h_send, h_recv, s_send, s_recv) = scratch[8:]
 
     t = lax.axis_index("tm")
     y = lax.axis_index("query")
@@ -260,12 +176,127 @@
 
     taps_n = kern_ref.shape[0]
     rim = taps_n // 2
+    halo = 2 * rim
     block = 8 * GROUPS
     ext = grad.shape[0]
+    tiles = e_ref.shape[0]
+    wide = x_ref.shape[0]
     lane = lax.broadcasted_iota(jnp.int32, (8, LANES), 1) + y * queries
 
+    def halo_copy(side):
+        device = {"tm": lax.rem(t + (tms - 1 if side == 0 else 1), tms)}
+        return copy(
+            halo_ref.at[side], hin.at[1 - side], h_send.at[side], h_recv.at[1 - side], device
+        )
+
+    has = [t > 0, t < tms - 1]
+    for side in range(2):
+        @pl.when(has[side])
+        def _(side=side):
+            halo_copy(side).start()
+
+    frame = lax.broadcasted_iota(jnp.int32, (wide, LANES), 0) + (t * row_count - halo)
+    valid_ref[...] = jnp.where((frame >= 0) & (frame < len_ref[0]), 1.0, 0.0)
+    x_ref[halo : halo + row_count, :] = fr_ref[...]
+    lab_ref[rim : rim + row_count, :] = own_lab_ref[...]
+    stat[...] = jnp.zeros_like(stat)
+    f_ref[...] = jnp.full_like(f_ref, -jnp.inf)
+
+    for side in range(2):
+        @pl.when(has[side])
+        def _(side=side):
+            halo_copy(1 - side).wait_recv()
+
+        @pl.when(jnp.logical_not(has[side]))
+        def _(side=side):
+            hin[side] = jnp.zeros((halo, hin.shape[2]), jnp.float32)
+
+    x_ref[:halo, :] = hin[0, :, :width].astype(jnp.bfloat16)
+    x_ref[halo + row_count :, :] = hin[1, :, :width].astype(jnp.bfloat16)
+    lab_ref[:rim, :] = hin[0, halo - rim :, width:]
+    lab_ref[rim + row_count :, :] = hin[1, :rim, width:]
+
+    def score(c, carry):
+        rows = pl.ds(pl.multiple_of(c * 2 * LANES, 2 * LANES), 2 * LANES)
+        part = lax.dot_general(
+            x_ref[...],
+            qu_ref[rows, :],
+            (((1,), (1,)), ((), ())),
+            preferred_element_type=jnp.float32,
+        )
+        for h in range(2):
+            one = part[:, h * LANES : (h + 1) * LANES] * scale
+            sc_ref[2 * c + h] = jnp.where(valid_ref[...] > 0, one, 0.0)
+        return carry
+
+    lax.fori_loop(0, tiles // 2, score, 0)
+
+    def smoothed(c, carry):
+        taps = spread_taps(kern_ref, at(c))
+
+        def body(g, carry):
+            base = pl.multiple_of(g * block, block)
+            sums = tap_block(lambda o: sc_ref[c, pl.ds(base + o, 8), :], taps, False)
+            for i in range(GROUPS):
+                rows = pl.ds(base + 8 * i, 8)
+                e_ref[c, rows, :] = sums[i]
+                f_ref[rows, :] = jnp.maximum(f_ref[rows, :], sums[i])
+            return carry
+
+        return lax.fori_loop(0, ext // block, body, carry)
+
+    lax.fori_loop(0, tiles, smoothed, 0)
+
+    diagonal = lax.broadcasted_iota(jnp.int32, (block, LANES), 0) == lax.broadcasted_iota(
+        jnp.int32, (block, LANES), 1
+    )
+
+    def finish(g, carry):
+        rows = pl.ds(pl.multiple_of(g * block, block), block)
+        top = jnp.max(f_ref[rows, :], axis=1, keepdims=True)
+        top = jnp.broadcast_to(top, (block, LANES))
+        total = jnp.zeros((block, LANES), jnp.float32)
+        for c in range(tiles):
+            e = jnp.exp(e_ref[c, rows, :] - top)
+            e_ref[c, rows, :] = e
+            total = total + e
+        total = jnp.broadcast_to(jnp.sum(total, axis=1, keepdims=True), (block, LANES))
+        for i, value in enumerate((top, total)):
+            picked = jnp.where(diagonal, value, 0.0)
+            stat[0, i, pl.ds(g, 1), :] = jnp.sum(picked, axis=0, keepdims=True)
+        return carry
+
+    lax.fori_loop(0, ext // block, finish, 0)
+
+    def stat_copy(k):
+        bit = lax.rem(y // (1 << k), 2)
+        device = {"query": y + (1 - 2 * bit) * (1 << k)}
+        return copy(stat.at[k], stat_in.at[k], s_send.at[k], s_recv.at[k], device)
+
+    rounds = peers.bit_length() - 1
+    for k in range(rounds):
+        stat_copy(k).start()
+        stat_copy(k).wait_recv()
+        top = jnp.maximum(stat[k, 0], stat_in[k, 0])
+        stat[k + 1, 0] = top
+        stat[k + 1, 1] = stat[k, 1] * jnp.exp(stat[k, 0] - top) + stat_in[k, 1] * jnp.exp(
+            stat_in[k, 0] - top
+        )
+    stat[rounds, 1] = jnp.exp(stat[0, 0] - stat[rounds, 0]) / stat[rounds, 1]
+
+    def widen(g, carry):
+        rows = pl.ds(pl.multiple_of(g * block, block), block)
+        row = jnp.broadcast_to(stat[rounds, 1, pl.ds(g, 1), :], (block, LANES))
+        factor = jnp.sum(jnp.where(diagonal, row, 0.0), axis=1, keepdims=True)
+        factor = jnp.broadcast_to(factor, (block, LANES))
+        valid = valid_ref[pl.ds(pl.multiple_of(g * block, block) + rim, block), :] > 0
+        f_ref[rows, :] = jnp.where(valid, factor, -1.0)
+        return carry
+
+    lax.fori_loop(0, ext // block, widen, 0)
+
     def map_gradient(c):
-        first = lane + c * chunk
+        first = (lane + c * chunk).astype(jnp.float32)
 
         def body(g, carry):
             for i in range(GROUPS):
@@ -386,19 +417,23 @@
     stages += [(k, functools.partial(exchange, k)) for k in range(bits - 1, 0, -1)]
 
     def step(s, carry):
-        @pl.when(s == count)
-        def _():
-            send_frames()
-
         for delay, stage in stages:
             @pl.when((s >= delay) & (s < count + delay))
             def _(stage=stage, delay=delay):
                 stage(s - delay)
+
+        @pl.when(s == count - 1)
+        def _():
+            send_frames()
+
+        @pl.when(s == count + 1)
+        def _():
+            f_compute(y)
+
         return carry
 
     lax.fori_loop(0, count + last_lag, step, 0)
 
-    f_compute(y)
     for d in range(1, peers):
         f_copy(d).wait_recv()
     total = fpart[y]
@@ -423,9 +458,15 @@
         return carry
 
     lax.fori_loop(0, count, drain, 0)
-
-
-def gradients(scores, exps, factor, labels, frame_rows, queries, kernel, scale):
+    for k in range(rounds):
+        stat_copy(k).wait_send()
+    for side in range(2):
+        @pl.when(has[side])
+        def _(side=side):
+            halo_copy(side).wait_send()
+
+
+def gradients(halo_rows, labels, lengths, frame_rows, queries, kernel, scale):
     tms, peers, recs = (lax.axis_size("tm"), lax.axis_size("query"), lax.axis_size("rec"))
     bits = recs.bit_length() - 1
     row_count, width = frame_rows.shape
@@ -434,6 +475,10 @@
     chunk = LANES
     count = query_count // chunk
     cols, fcols = (width // recs, width // peers)
+    rim = taps // 2
+    ext, wide = (row_count + 2 * rim, row_count + 4 * rim)
+    rounds = peers.bit_length() - 1
+    stat_rows = (ext // (8 * GROUPS) + 7) // 8 * 8
     f32 = jnp.float32
     small = pltpu.VMEM((count, taps, chunk), f32)
     block = pltpu.VMEM((query_count, cols), f32)
@@ -444,11 +489,21 @@
         pltpu.VMEM((peers, row_count, fcols), f32),
         pltpu.VMEM((peers - 1, row_count, fcols), f32),
         pltpu.VMEM((row_count, query_count), jnp.bfloat16),
-        pltpu.VMEM((exps.shape[1], chunk), f32),
+        pltpu.VMEM((ext, chunk), f32),
         pltpu.VMEM((taps, chunk), f32),
+        pltpu.VMEM((count, wide, chunk), f32),
+        pltpu.VMEM((count, ext, chunk), f32),
+        pltpu.VMEM((ext, chunk), f32),
+        pltpu.VMEM((ext, chunk), f32),
+        pltpu.VMEM((wide, chunk), f32),
+        pltpu.VMEM((wide, width), jnp.bfloat16),
+        pltpu.VMEM(halo_rows.shape, f32),
+        pltpu.VMEM((rounds + 1, 2, stat_rows, LANES), f32),
+        pltpu.VMEM((rounds, 2, stat_rows, LANES), f32),
     ]
     dma = pltpu.SemaphoreType.DMA
     scratch += [dma((bits, 2, count))] * 2 + [dma((2, count))] * 4 + [dma((peers - 1,))] * 2
+    scratch += [dma((2,))] * 2 + [dma((rounds,))] * 2
     vmem = pl.BlockSpec(memory_space=pltpu.VMEM)
     return pl.pallas_call(
         functools.partial(gradient_kernel, (tms, peers, recs, chunk), scale),
@@ -457,71 +512,31 @@
             jax.ShapeDtypeStruct((query_count, cols), jnp.bfloat16),
             jax.ShapeDtypeStruct((taps, query_count), f32),
         ),
-        in_specs=[vmem] * 7,
+        in_specs=[vmem, vmem, pl.BlockSpec(memory_space=pltpu.SMEM), vmem, vmem, vmem],
         out_specs=(vmem,) * 3,
         scratch_shapes=scratch,
         compiler_params=pltpu.CompilerParams(
             collective_id=0, has_side_effects=True, vmem_limit_bytes=60 * 1024 * 1024
         ),
         name="gradients",
-    )(scores, exps, factor, labels, frame_rows, queries, kernel)
-
-
-def combine_stats(first_pair, second_pair):
-    top_value = jnp.maximum(first_pair[0], second_pair[0])
-    total_value = first_pair[1] * jnp.exp(first_pair[0] - top_value) + second_pair[1] * jnp.exp(
-        second_pair[0] - top_value
-    )
-    return jnp.stack([top_value, total_value])
+    )(halo_rows, labels, lengths, frame_rows, queries, kernel)
 
 
 def per_device(frames, queries, kernel, labels, lengths):
     frame_rows = frames[0]
-    label_ids = labels[0]
-    length_now = lengths[0]
-    row_count = frame_rows.shape[0]
-    query_count = queries.shape[0]
-    width = frame_rows.shape[1]
-    tap_count = kernel.shape[0]
-    rim_width = tap_count // 2
+    row_count, width = frame_rows.shape
+    halo = kernel.shape[0] // 2 * 2
     logit_scale = 10.0 / math.sqrt(width)
-    frame_start = lax.axis_index("tm") * row_count
-    halo = 2 * rim_width
-    tagged = jnp.concatenate(
+    label_wide = jnp.broadcast_to(labels[0].astype(jnp.float32)[:, None], (row_count, LANES))
+    ends = (slice(0, halo), slice(row_count - halo, row_count))
+    halo_rows = jnp.stack(
         [
-            frame_rows.astype(jnp.float32),
-            jnp.broadcast_to(label_ids.astype(jnp.float32)[:, None], (row_count, 128)),
-        ],
-        axis=1,
-    )
-    before, after = halo_rows(tagged, "tm", halo)
-    rim_rows = jnp.concatenate([before[:, :width], after[:, :width]]).astype(jnp.bfloat16)
-
-    wide_rows = jnp.concatenate([rim_rows[:halo], frame_rows, rim_rows[halo:]])
-    wide_frames = frame_start - halo + jnp.arange(row_count + 2 * halo, dtype=jnp.int32)
-    wide_valid = (wide_frames >= 0) & (wide_frames < length_now)
-    wide_valid = jnp.broadcast_to(wide_valid[:, None], (wide_valid.shape[0], LANES))
-    label_pad = jnp.concatenate(
-        [
-            before[halo - rim_width :, width].astype(jnp.int32),
-            label_ids,
-            after[:rim_width, width].astype(jnp.int32),
+            jnp.concatenate([frame_rows[rows].astype(jnp.float32), label_wide[rows]], axis=1)
+            for rows in ends
         ]
     )
-    ext_rows = row_count + 2 * rim_width
-    ext_frames = frame_start - rim_width + jnp.arange(ext_rows, dtype=jnp.int32)
-    ext_valid = (ext_frames >= 0) & (ext_frames < length_now)
-    scores, exps, local_top, local_total = smooth_exp(
-        wide_rows, queries, kernel, wide_valid.astype(jnp.float32), logit_scale
-    )
-    top = local_top[:, 0]
-    stats = merged(jnp.stack([top, local_total[:, 0]]), "query", combine_stats)
-    factor = jnp.exp(top - stats[0]) / stats[1]
-    factor = jnp.where(ext_valid, factor, -1.0)
-    factor = jnp.broadcast_to(factor[:, None], (ext_rows, LANES))
-    label_wide = jnp.broadcast_to(label_pad[:, None], (ext_rows, LANES))
     grad_frames, grad_queries, grad_kernel = gradients(
-        scores, exps, factor, label_wide, frame_rows, queries, kernel, logit_scale
+        halo_rows, label_wide, lengths, frame_rows, queries, kernel, logit_scale
     )
     return (grad_frames[None], grad_queries, grad_kernel)
 

time: 140 us -> 124 us (0.89)
  starting transfers between devices: 8.75 us -> 0 us
  local copies, waits for them, and re-layouts: 11.7 us -> 6.9 us
  waiting for transfers between devices: 4.28 us -> 0 us
  Pallas kernels: 110 us -> 114 us
    pallas_call x1, Pallas kernels: 88 us -> 114 us  [gradients(): pl.pallas_call(functools.partial(gradient_kernel, (tms, peers, recs, chun...]
    pallas_call x1 -> x0, Pallas kernels: 22.5 us -> none  [smooth_exp(): pl.pallas_call(functools.partial(smooth_kernel, scale), out_shape=(jax.Sh...]
    ppermute x3 -> x0, starting transfers between devices: 8.75 us -> none  [the longest x1 5.59 us: halo_rows(): before = lax.ppermute(x[x.shape[0] - width:], axis, up)]
    ppermute x3 -> x0, waiting for transfers between devices: 4.28 us -> none  [the longest x1 1.87 us: merged(): x = combine(x, lax.ppermute(x, axis, swap))]
    unnamed x15 -> x3, local copies, waits for them, and re-layouts: 9.21 us -> 5.85 us
  transfers between devices with their start and end apart: 3 -> 0, of which waited for: 3 -> 0; matrix products, arithmetic and copies ran while one was open for 0% -> 0% of each run, Pallas kernels for 0% -> 0%
where the time goes in v4:
time: 124 us
  Pallas kernels  114 us (92%)
  local copies, waits for them, and re-layouts  6.9 us (6%)
  other arithmetic  2.33 us (2%)
  between operations  1.3 us (1%)
    pallas_call x1, Pallas kernels, gradients(): pl.pallas_call(functools.partial(gradient_kernel, (tms, peers, recs, chun...  114 us
    unnamed x3, local copies, waits for them, and re-layouts  5.85 us

profile of v4, /device:TPU:0, one launch (start us, length us, event | category | flops | bytes accessed | tf_op | source)
XLA Modules:
  0.0 124.1 jit_solution(1030983743957685050)
XLA Ops:
  1.3 0.7 convert_element_type.29
  2.0 0.1 slice_bitcast_fusion.1
  2.0 0.1 broadcast_in_dim.13
  2.1 0.1 broadcast_in_dim.14
  2.2 0.8 broadcast_in_dim.15.own_lab_ref
  3.0 0.9 bitcast_convert_fusion.1
  3.9 0.7 pad_maximum_fusion.halo_ref
  4.7 113.6 %gradients.1 = (bf16[512,512]{1,0:T(8,128)(2,1)}, bf16[2048,256]{1,0:T(8,128)(2,1)}, f32[33,2048]{1,0:T(8,128)}) custom-call(f32[2,32,1152]{2,1,0:T(8,128)} %pad_maximum_fusion.halo_ref, f32[512,128]{1,0:T(8,128)} %broadcast_in_dim.15.own_lab_ref, s32[1]{0:T(128)S(6)} %copy.11.len_ref, bf16[512,1024]{1,0:T(8,128)(2,1)} %bitcast.17, ...), custom_call_target="tpu_custom_call" | custom-call | tf_op jit(solution)/shard_map/gradients/pallas_call | solution.py:508
  118.3 1.9 %copy.12 = bf16[1,512,512]{2,1,0:T(8,128)(2,1)} copy(bf16[1,512,512]{2,1,0:T(8,128)(2,1)} %bitcast.18) | data formatting | bytes 1048576
  120.1 2.3 %copy.13 = bf16[2048,256]{1,0:T(8,128)(2,1)} copy(bf16[2048,256]{1,0:T(8,128)(2,1)} %get-tuple-element.19) | data formatting | bytes 2097152
  122.4 1.7 %copy.14 = f32[33,2048]{1,0:T(8,128)} copy(f32[33,2048]{1,0:T(8,128)} %get-tuple-element.20) | data formatting | bytes 540672
  (1 shorter events, 0.0 us)

commit v5 on v4

--- a/solution.py
+++ b/solution.py
@@ -41,7 +41,6 @@
 def gradient_kernel(
     dims,
     scale,
-    halo_ref,
     own_lab_ref,
     len_ref,
     fr_ref,
@@ -59,8 +58,8 @@
     kacc, scratch = scratch[:bits], scratch[bits:]
     karrived, scratch = scratch[:bits], scratch[bits:]
     (mid, outer, inner, kmid, kouter, kinner, fpart, fin, sg_ref, grad, ksum) = scratch[:11]
-    (sc_ref, e_ref, f_ref, lab_ref, valid_ref, x_ref, hin, stat, stat_in) = scratch[11:20]
-    scratch = scratch[20:]
+    (sc_ref, e_ref, f_ref, lab_ref, valid_ref, x_ref, hin, hout, stat, stat_in) = scratch[11:21]
+    scratch = scratch[21:]
     (rec_send, rec_recv, in_send, out_recv, out_send, inn_recv, f_send, f_recv) = scratch[:8]
     (h_send, h_recv, s_send, s_recv) = scratch[8:]
 
@@ -186,8 +185,13 @@
     def halo_copy(side):
         device = {"tm": lax.rem(t + (tms - 1 if side == 0 else 1), tms)}
         return copy(
-            halo_ref.at[side], hin.at[1 - side], h_send.at[side], h_recv.at[1 - side], device
-        )
+            hout.at[side], hin.at[1 - side], h_send.at[side], h_recv.at[1 - side], device
+        )
+
+    for side, begin in enumerate((0, row_count - halo)):
+        rows = slice(begin, begin + halo)
+        hout[side, :, :width] = fr_ref[rows, :].astype(jnp.float32)
+        hout[side, :, width:] = own_lab_ref[rows, :].astype(jnp.float32)
 
     has = [t > 0, t < tms - 1]
     for side in range(2):
@@ -198,7 +202,7 @@
     frame = lax.broadcasted_iota(jnp.int32, (wide, LANES), 0) + (t * row_count - halo)
     valid_ref[...] = jnp.where((frame >= 0) & (frame < len_ref[0]), 1.0, 0.0)
     x_ref[halo : halo + row_count, :] = fr_ref[...]
-    lab_ref[rim : rim + row_count, :] = own_lab_ref[...]
+    lab_ref[rim : rim + row_count, :] = own_lab_ref[...].astype(jnp.float32)
     stat[...] = jnp.zeros_like(stat)
     f_ref[...] = jnp.full_like(f_ref, -jnp.inf)
 
@@ -466,7 +470,7 @@
             halo_copy(side).wait_send()
 
 
-def gradients(halo_rows, labels, lengths, frame_rows, queries, kernel, scale):
+def gradients(labels, lengths, frame_rows, queries, kernel, scale):
     tms, peers, recs = (lax.axis_size("tm"), lax.axis_size("query"), lax.axis_size("rec"))
     bits = recs.bit_length() - 1
     row_count, width = frame_rows.shape
@@ -497,7 +501,8 @@
         pltpu.VMEM((ext, chunk), f32),
         pltpu.VMEM((wide, chunk), f32),
         pltpu.VMEM((wide, width), jnp.bfloat16),
-        pltpu.VMEM(halo_rows.shape, f32),
+        pltpu.VMEM((2, 2 * rim, width + LANES), f32),
+        pltpu.VMEM((2, 2 * rim, width + LANES), f32),
         pltpu.VMEM((rounds + 1, 2, stat_rows, LANES), f32),
         pltpu.VMEM((rounds, 2, stat_rows, LANES), f32),
     ]
@@ -512,31 +517,23 @@
             jax.ShapeDtypeStruct((query_count, cols), jnp.bfloat16),
             jax.ShapeDtypeStruct((taps, query_count), f32),
         ),
-        in_specs=[vmem, vmem, pl.BlockSpec(memory_space=pltpu.SMEM), vmem, vmem, vmem],
+        in_specs=[vmem, pl.BlockSpec(memory_space=pltpu.SMEM), vmem, vmem, vmem],
         out_specs=(vmem,) * 3,
         scratch_shapes=scratch,
         compiler_params=pltpu.CompilerParams(
             collective_id=0, has_side_effects=True, vmem_limit_bytes=60 * 1024 * 1024
         ),
         name="gradients",
-    )(halo_rows, labels, lengths, frame_rows, queries, kernel)
+    )(labels, lengths, frame_rows, queries, kernel)
 
 
 def per_device(frames, queries, kernel, labels, lengths):
     frame_rows = frames[0]
     row_count, width = frame_rows.shape
-    halo = kernel.shape[0] // 2 * 2
     logit_scale = 10.0 / math.sqrt(width)
-    label_wide = jnp.broadcast_to(labels[0].astype(jnp.float32)[:, None], (row_count, LANES))
-    ends = (slice(0, halo), slice(row_count - halo, row_count))
-    halo_rows = jnp.stack(
-        [
-            jnp.concatenate([frame_rows[rows].astype(jnp.float32), label_wide[rows]], axis=1)
-            for rows in ends
-        ]
-    )
+    label_wide = jnp.broadcast_to(labels[0][:, None], (row_count, LANES))
     grad_frames, grad_queries, grad_kernel = gradients(
-        halo_rows, label_wide, lengths, frame_rows, queries, kernel, logit_scale
+        label_wide, lengths, frame_rows, queries, kernel, logit_scale
     )
     return (grad_frames[None], grad_queries, grad_kernel)
 

time: 124 us -> 122 us (0.984)
  other arithmetic: 2.33 us -> 0 us
    convert_element_type x2 -> x0, other arithmetic: 1.57 us -> none  [the longest x1 0.89 us: per_device(): frame_rows[rows].astype(jnp.float32)]
where the time goes in v5:
time: 122 us
  Pallas kernels  114 us (93%)
  local copies, waits for them, and re-layouts  7.37 us (6%)
  between operations  1.29 us (1%)
    pallas_call x1, Pallas kernels, gradients(): pl.pallas_call(functools.partial(gradient_kernel, (tms, peers, recs, chun...  114 us
    unnamed x3, local copies, waits for them, and re-layouts  5.85 us

profile of v5, /device:TPU:0, one launch (start us, length us, event | category | flops | bytes accessed | tf_op | source)
XLA Modules:
  0.0 122.2 jit_solution(12281221673126075320)
XLA Ops:
  1.3 1.5 %broadcast_in_dim.11.own_lab_ref = s32[512,128]{1,0:T(8,128)} broadcast(s32[512]{0:T(512)} %bitcast.5), dimensions={0} | broadcast | bytes 264192 | tf_op jit(solution)/shard_map/broadcast_in_dim | solution.py:534
  2.8 113.5 %gradients.1 = (bf16[512,512]{1,0:T(8,128)(2,1)}, bf16[2048,256]{1,0:T(8,128)(2,1)}, f32[33,2048]{1,0:T(8,128)}) custom-call(s32[512,128]{1,0:T(8,128)} %broadcast_in_dim.11.own_lab_ref, s32[1]{0:T(128)S(6)} %copy.11.len_ref, bf16[512,1024]{1,0:T(8,128)(2,1)} %bitcast.3, bf16[2048,1024]{1,0:T(8,128)(2,1)} %qu_ref.1, f32[33,2048]{1,0:T(8,128)} %kern_ref.1), custom_call_target="tpu_custom_call" | custom-call | tf_op jit(solution)/shard_map/gradients/pallas_call | solution.py:513
  116.3 1.9 %copy.12 = bf16[1,512,512]{2,1,0:T(8,128)(2,1)} copy(bf16[1,512,512]{2,1,0:T(8,128)(2,1)} %bitcast.4) | data formatting | bytes 1048576
  118.2 2.3 %copy.13 = bf16[2048,256]{1,0:T(8,128)(2,1)} copy(bf16[2048,256]{1,0:T(8,128)(2,1)} %get-tuple-element.13) | data formatting | bytes 2097152
  120.5 1.7 %copy.14 = f32[33,2048]{1,0:T(8,128)} copy(f32[33,2048]{1,0:T(8,128)} %get-tuple-element.14) | data formatting | bytes 540672
